TPU v7x, 32 devices: a whole 2x2x4 slice. The times are simulated.
32 devices in a mesh: parts: 2 (over x), limb: 8 (over z, y), rot: 2 (over core).
Axes of the slice: x: 2, y: 2, z: 4, core: 2. Of those that a mesh axis runs over, the one named last changes fastest.
Arguments:
- cipher: float32 [64, 65536], P(('parts', 'limb')), parts along dimension 0, may hold values from -6 to 6
- rotation_keys: float32 [2, 4, 3, 2, 32, 65536], P('rot', None, None, None, 'limb'), may hold values from -3.5 to 3.5
- diagonals: float32 [2, 4, 32, 65536], P('rot', None, 'limb'), may hold values from -2 to 2
- shifts: int32 [2, 4], P('rot'), may hold values from 1 to 65535
- twiddles: int32 [32], replicated, may hold values from 1 to 255, as said below
- moduli: int32 [32], replicated, may hold values from 1048576 to 2097151
- digit_of: int32 [32], replicated, may hold values from 0 to 3, as said below
- conversion: float32 [32, 32], replicated, may hold values from -2 to 2
Outputs:
- product: float32 [2, 64, 65536], P(None, ('parts', 'limb'), 'rot'), parts along dimension 1
There are 2 independent parts, one for each index of `parts`. A program takes and returns all parts, laid end to end along the dimension named above; an argument that names none is the same for every part. Nothing has to cross between parts.
Inputs may be any that keep to these rules, and one draw needn't show every extreme that they name: `digit_of`: each of the 3 digits and the special value 3 is taken by exactly 8 limbs. `twiddles`: odd.
All inputs are finite; a program needn't handle non-finite values.
Results may differ from a plain program's by a relative error of at most 0.0003.
Values sent between devices are 32-bit elements; how exact they have to be, the bound alone decides.
No kernel may reach another device: no remote copies, remote signals or barrier semaphores. Data moves between devices by JAX's collectives and lax.ppermute only.
A program may use at most 256 MiB of HBM per device.

v0:
```python
import functools
import math

import jax
import jax.numpy as jnp
import numpy as np
from jax import lax
from jax.experimental import pallas as pl
from jax.experimental.pallas import tpu as pltpu
from jax.sharding import PartitionSpec as P

RADIX = 256
DIGITS = 3
LANES = 128
PLAN = 4
F32 = jnp.float32
BF16 = jnp.bfloat16


ANY = pl.BlockSpec(memory_space=pl.ANY)
VMEM = pl.BlockSpec(memory_space=pltpu.VMEM)
HBM = pl.BlockSpec(memory_space=pltpu.HBM)
SMEM = pl.BlockSpec(memory_space=pltpu.SMEM)


def ring_order(mesh):
    n = mesh.shape["limb"]
    line = np.moveaxis(mesh.devices, list(mesh.axis_names).index("limb"), 0).reshape(n, -1)[:, 0]
    at = [getattr(d, "coords", None) for d in line]
    if any(c is None for c in at):
        return list(range(n))
    near = [
        [j for j in range(n) if sum(abs(x - y) for x, y in zip(at[i], at[j])) == 1] for i in range(n)
    ]

    def walk(path):
        if len(path) == n:
            return path if 0 in near[path[-1]] else None
        for j in near[path[-1]]:
            if j not in path:
                found = walk(path + [j])
                if found:
                    return found
        return None

    return walk([0]) or list(range(n))


def split(x):
    hi = x.astype(BF16)
    return hi, (x - hi.astype(F32)).astype(BF16)


def mm(a, b):
    dot = functools.partial(jnp.dot, preferred_element_type=F32)
    return dot(a[0], b[0]) + dot(a[1], b[0]) + dot(a[0], b[1])


def spin(x, h):
    return mm(h, split(mm(split(x), h)))


def grid_of(ref, m, limbs):
    left = ref[pl.ds(m, RADIX, stride=2 * limbs), :]
    right = ref[pl.ds(limbs + m, RADIX, stride=2 * limbs), :]
    return jnp.concatenate([left, right], axis=1)


def in_hbm(x):
    return pltpu.with_memory_space_constraint(x, pltpu.HBM)


def params(mib):
    return pltpu.CompilerParams(vmem_limit_bytes=mib * 2**20)


def coef_kernel(start, limbs, tw, where, base_hi, base_lo, cipher, *refs):
    coef, mats, grid, bases, sem = refs[-5:]
    copies = [
        pltpu.make_async_copy(base_hi, bases.at[0], sem.at[0]),
        pltpu.make_async_copy(base_lo, bases.at[1], sem.at[1]),
        pltpu.make_async_copy(cipher, grid, sem.at[2]),
    ]
    for copy in copies:
        copy.start()
    row = lax.broadcasted_iota(jnp.int32, (RADIX, RADIX), 0)
    col = lax.broadcasted_iota(jnp.int32, (RADIX, RADIX), 1)
    first = where[1] == 0
    if start:
        mats[:start] = refs[0][...]
    for copy in copies:
        copy.wait()
    for i in range(coef.shape[0]):
        m = start + i
        g = tw[where[0] * limbs + m]
        pick = jnp.where(((row * g) & (RADIX - 1)) == col, 1.0, 0.0).astype(BF16)
        hi = jnp.dot(pick, bases[0], preferred_element_type=F32).astype(BF16)
        lo = jnp.dot(pick, bases[1], preferred_element_type=F32).astype(BF16)
        mats[m, 0] = hi
        mats[m, 1] = lo
        u = split(mm((hi, lo), split(grid_of(grid, m, limbs))))
        half = tuple(
            jnp.where(first, h[:, :LANES].astype(F32), h[:, LANES:].astype(F32)).astype(BF16) for h in (hi, lo)
        )
        coef[i] = mm(u, half)


def coef_call(start, stop, limbs, tw, where, base_hi, base_lo, cipher, before=()):
    return pl.pallas_call(
        functools.partial(coef_kernel, start, limbs),
        in_specs=[SMEM, SMEM, HBM, HBM, HBM] + [VMEM] * len(before),
        out_specs=[VMEM, VMEM],
        out_shape=[
            jax.ShapeDtypeStruct((stop - start, RADIX, LANES), F32),
            jax.ShapeDtypeStruct((stop, 2, RADIX, RADIX), BF16),
        ],
        scratch_shapes=[
            pltpu.VMEM(cipher.shape, F32),
            pltpu.VMEM((2, RADIX, RADIX), BF16),
            pltpu.SemaphoreType.DMA((3,)),
        ],
        compiler_params=params(12),
        cost_estimate=pl.CostEstimate(flops=10**9, bytes_accessed=2**20, transcendentals=0),
        name="coef",
    )(in_hbm(tw), where, in_hbm(base_hi), in_hbm(base_lo), in_hbm(cipher), *before)


def mix_kernel(limbs, lens, order, digit, where, srcs, conv, *refs):
    blocks, out, got, table, sem = refs[: len(lens)], refs[-4], refs[-3], refs[-2], refs[-1]
    size = got.shape[0] * limbs // (DIGITS + 1)
    copies = []
    for i, (start, stop) in enumerate(lens):
        c = pltpu.make_async_copy(blocks[i], got.at[srcs[i], pl.ds(start, stop - start)], sem.at[i])
        c.start()
        copies.append(c)
    first = where[0] * limbs
    for j in range(DIGITS * size):
        l = order[j]
        for m in range(limbs):
            same = digit[l] == digit[first + m]
            one = jnp.where(first + m == l, 1.0, 0.0)
            table[m, j] = jnp.where(same, one, conv[first + m, l])
    for c in copies:
        c.wait()
    step = 64

    def rows(r, carry):
        r0 = pl.multiple_of(r * step, step)
        for d in range(DIGITS):
            acc = [jnp.zeros((step, LANES), F32) for _ in range(limbs)]
            for j in range(size):
                l = order[d * size + j]
                x = got[l // limbs, l % limbs, pl.ds(r0, step), :]
                for m in range(limbs):
                    acc[m] = acc[m] + table[m, d * size + j] * x
            for m in range(limbs):
                out[d, m, pl.ds(r0, step), :] = acc[m]
        return carry

    lax.fori_loop(0, RADIX // step, rows, 0)


def mix_call(n, limbs, lens, order, digit, where, srcs, conv, blocks):
    vmem = pl.BlockSpec(memory_space=pltpu.VMEM)
    return pl.pallas_call(
        functools.partial(mix_kernel, limbs, lens),
        in_specs=[SMEM] * 5 + [HBM] * len(blocks),
        out_specs=vmem,
        out_shape=jax.ShapeDtypeStruct((DIGITS, limbs, RADIX, LANES), F32),
        scratch_shapes=[
            pltpu.VMEM((n, limbs, RADIX, LANES), F32),
            pltpu.SMEM((limbs, n * limbs), F32),
            pltpu.SemaphoreType.DMA((len(blocks),)),
        ],
        compiler_params=params(16),
        name="mix",
    )(order, in_hbm(digit), where, srcs, in_hbm(conv), *blocks)


def raise_kernel(pad, digit, where, own, other, mats, cipher, out, rows_in, sem):
    limbs = mats.shape[0]
    rows = cipher.shape[0]
    swapped = where[1] != 0
    fetch = pltpu.make_async_copy(cipher, rows_in, sem)
    fetch.start()

    def at(m, h):
        return pl.ds(h * limbs + m, RADIX, stride=2 * limbs)

    def convert(m, carry):
        h = (mats[m, 0], mats[m, 1])
        for d in range(DIGITS):
            a, b = own[d, m], other[d, m]
            x = jnp.concatenate([jnp.where(swapped, b, a), jnp.where(swapped, a, b)], axis=1)
            y = spin(x, h)
            for i in range(2):
                out[d, at(m, i), :] = y[:, i * LANES : (i + 1) * LANES]
        return carry

    lax.fori_loop(0, limbs, convert, 0)
    fetch.wait()

    def place(m, carry):
        d = digit[where[0] * limbs + m]
        for h in range(2):
            out[d, at(m, h), :] = rows_in[at(m, h), :]

        @pl.when(d != DIGITS)
        def _():
            for h in range(2):
                out[DIGITS, at(m, h), :] = jnp.zeros((RADIX, LANES), F32)

        return carry

    lax.fori_loop(0, limbs, place, 0)
    for d in range(DIGITS + 1):
        out[d, pl.ds(rows, pad), :] = out[d, pl.ds(0, pad), :]


def raise_call(digit, where, own, other, mats, cipher, pad):
    rows = cipher.shape[0]
    return pl.pallas_call(
        functools.partial(raise_kernel, pad),
        in_specs=[SMEM, SMEM] + [VMEM] * 3 + [HBM],
        out_specs=VMEM,
        out_shape=jax.ShapeDtypeStruct((DIGITS + 1, rows + pad, LANES), F32),
        scratch_shapes=[pltpu.VMEM(cipher.shape, F32), pltpu.SemaphoreType.DMA],
        compiler_params=params(16),
        name="raise",
    )(in_hbm(digit), where, own, other, mats, in_hbm(cipher))


def accum_kernel(k, limbs, pad, shifts, raised, keys, diag, gain, *refs):
    part, acc, kbuf, dbuf, small, sem, ksem = refs[-8:-6], *refs[-6:]
    rows = acc.shape[1]
    pieces = ksem.shape[0]
    block = rows // pieces

    def fetch(i):
        at = pl.ds(pl.multiple_of(i * block, block), block)
        return [
            pltpu.make_async_copy(keys.at[k, :, at], kbuf.at[:, at], ksem.at[i, 0]),
            pltpu.make_async_copy(diag.at[k, at], dbuf.at[at], ksem.at[i, 1]),
        ]

    amounts = pltpu.make_async_copy(shifts, small, sem)
    amounts.start()
    for i in range(pieces):
        for copy in fetch(i):
            copy.start()
    amounts.wait()
    s = small[0, k]
    tiles, lane = s // LANES, s % LANES
    here = lax.broadcasted_iota(jnp.int32, (pad, LANES), 1) < LANES - lane
    g8 = jnp.concatenate([gain[...]] * (pad // 8), axis=0)

    def piece(i, carry):
        for copy in fetch(i):
            copy.wait()

        def add(r, carry):
            at = pl.multiple_of(i * block + r * pad, pad)
            u0 = lax.rem(at - limbs * tiles + rows, rows)
            v0 = lax.rem(at - limbs * tiles - limbs + 2 * rows, rows)
            turned = []
            for g in range(DIGITS + 1):
                u = raised[g, pl.ds(pl.multiple_of(u0, limbs), pad), :]
                v = raised[g, pl.ds(pl.multiple_of(v0, limbs), pad), :]
                turned.append(pltpu.roll(jnp.where(here, u, v), lane, axis=1))
            w = dbuf[pl.ds(at, pad), :] * g8
            for c in range(2):
                a = turned[DIGITS]
                for d in range(DIGITS):
                    a = a + turned[d] * kbuf[2 * d + c, pl.ds(at, pad), :]
                acc[c, pl.ds(at, pad), :] = a
                w_a = w * a
                part[c][pl.ds(at, pad), :] = w_a if k == 0 else refs[c][pl.ds(at, pad), :] + w_a
            return carry

        return lax.fori_loop(0, block // pad, add, carry, unroll=2)

    lax.fori_loop(0, pieces, piece, 0)


def accum_call(k, shifts, raised, keys, diag, gain, limbs, pad, part):
    rows = raised.shape[1] - pad
    args = (in_hbm(shifts), raised, in_hbm(keys), in_hbm(diag), gain)
    specs = [HBM, VMEM, HBM, HBM, VMEM]
    alias = {}
    if part is not None:
        alias = {len(args) + i: i for i in range(2)}
        args += tuple(part)
        specs += [VMEM, VMEM]
    one = jax.ShapeDtypeStruct((rows, LANES), F32)
    return pl.pallas_call(
        functools.partial(accum_kernel, k, limbs, pad),
        in_specs=specs,
        out_specs=[VMEM, VMEM, VMEM],
        out_shape=[one, one, jax.ShapeDtypeStruct((2, rows, LANES), F32)],
        input_output_aliases=alias,
        scratch_shapes=[
            pltpu.VMEM(keys.shape[1:], F32),
            pltpu.VMEM((rows, LANES), F32),
            pltpu.SMEM(shifts.shape, jnp.int32),
            pltpu.SemaphoreType.DMA,
            pltpu.SemaphoreType.DMA((8, 2)),
        ],
        compiler_params=params(12),
        cost_estimate=pl.CostEstimate(flops=10**8, bytes_accessed=8 * 2**20, transcendentals=0),
        name="accum",
    )(*args)


def emit_kernel(k, limbs, specials, slot, acc, mats, *refs):
    store, stage, sem = refs[-4:-2], refs[-2], refs[-1]

    def emit(m, carry):
        @pl.when(slot[m] >= 0)
        def _():
            h = (mats[m, 0], mats[m, 1])
            copies = []
            for c in range(2):
                y = spin(grid_of(acc.at[c], m, limbs), h)
                stage[c, 0:RADIX, :] = y[:, :LANES]
                stage[c, RADIX:, :] = y[:, LANES:]
                copies.append(pltpu.make_async_copy(stage.at[c], store[c].at[k * specials + slot[m]], sem.at[c]))
                copies[-1].start()
            for copy in copies:
                copy.wait()

        return carry

    lax.fori_loop(0, limbs, emit, 0)


def emit_call(k, slot, acc, mats, specials, items, store):
    one = jax.ShapeDtypeStruct((items, 2 * RADIX, LANES), F32)
    args, specs, alias = (slot, acc, mats), [SMEM, VMEM, VMEM], {}
    if store is not None:
        alias = {len(args) + i: i for i in range(2)}
        args += tuple(map(in_hbm, store))
        specs += [HBM, HBM]
    return pl.pallas_call(
        functools.partial(emit_kernel, k, mats.shape[0], specials),
        in_specs=specs,
        out_specs=[HBM, HBM],
        out_shape=[one, one],
        input_output_aliases=alias,
        scratch_shapes=[pltpu.VMEM((2, 2 * RADIX, LANES), F32), pltpu.SemaphoreType.DMA((2,))],
        compiler_params=params(8),
        cost_estimate=pl.CostEstimate(flops=10**9, bytes_accessed=2**20, transcendentals=0),
        name="emit",
    )(*args)


def table_kernel(n, count, specials, limbs, least, order, pos, spot, plan, rounds, comp, a_ref, b_ref, end_ref):
    items = count * specials
    shape = (items, LANES)
    row_i = lax.broadcasted_iota(jnp.int32, shape, 0)
    row = row_i.astype(F32)
    lane = lax.broadcasted_iota(jnp.int32, shape, 1).astype(F32)
    kind, turn = lax.rem(row_i, specials), lax.div(row_i, specials)
    ready = jnp.maximum(2 * turn - 1, 0)
    weight = 3.0 * turn.astype(F32)
    p = spot[0]
    before, after = lax.rem(p + n - 1, n), lax.rem(p + 1, n)
    line = lax.broadcasted_iota(jnp.int32, (1, LANES), 1)
    org = jnp.zeros(shape, F32)
    for s in range(specials):
        owner = pos[lax.div(order[DIGITS * specials + s], limbs)]
        org = jnp.where(kind == s, owner.astype(F32), org)
    a_ref[...] = jnp.zeros(shape, F32)
    b_ref[...] = jnp.zeros(shape, F32)
    end_ref[...] = jnp.zeros(shape, F32)
    big = float(items * (2 * n + 3 * count))

    def choose(front, spread, t):
        open_ = jnp.logical_and(spread < n - 1, ready <= t)
        cand = jnp.logical_and(open_, front == lane)
        key = jnp.where(cand, (2.0 * spread + weight) * items + row, big)
        best = jnp.min(key, axis=0, keepdims=True)
        hit = jnp.where(jnp.logical_and(cand, key == best), 1.0, 0.0)
        item = jnp.sum(hit * (row - items), axis=0, keepdims=True) + items
        return item, jnp.sum(hit, axis=1, keepdims=True)

    def note(t, r, item, where):
        t = jnp.asarray(t, jnp.int32)
        mine = jnp.sum(jnp.where(line == where, item, 0.0), axis=1, keepdims=True)
        at = pl.ds(lax.div(PLAN * t + r, LANES), 1)
        here = line == lax.rem(PLAN * t + r, LANES)
        plan[at, :] = jnp.where(here, jnp.broadcast_to(mine, (1, LANES)).astype(jnp.int32), plan[at, :])

    none = jnp.full((1, LANES), float(items), F32)
    plan[...] = jnp.full(plan.shape, items, jnp.int32)
    note(0, 2, none, p)
    note(0, 3, none, p)

    def step(t, carry):
        a, b = a_ref[...], b_ref[...]
        front = org + a
        item, right = choose(jnp.where(front >= n, front - n, front), a + b, t)
        note(t, 0, item, p)
        note(t + 1, 2, item, before)
        a = a + right
        front = org - b
        item, left = choose(jnp.where(front < 0, front + n, front), a + b, t)
        note(t, 1, item, p)
        note(t + 1, 3, item, after)
        b = b + left
        a_ref[...] = a
        b_ref[...] = b
        end_ref[...] = jnp.where(right + left > 0, (t + 1).astype(F32), end_ref[...])
        return carry

    def missing():
        return jnp.sum(n - 1 - a_ref[...] - b_ref[...]).astype(jnp.int32)

    def more(c):
        step(c[0], 0)
        return c[0] + 1, missing()

    lax.fori_loop(0, least, step, 0)
    t, _ = lax.while_loop(lambda c: c[1] > 0, more, (jnp.int32(least), missing()))
    rounds[0] = t
    note(t, 0, none, p)
    note(t, 1, none, p)
    for k in range(count):
        comp[k] = jnp.max(end_ref[pl.ds(k * specials, specials), :]).astype(jnp.int32)


def table_call(n, count, specials, limbs, least, order, pos, spot):
    items = count * specials
    most = items * (n - 1) + 2 * count
    return pl.pallas_call(
        functools.partial(table_kernel, n, count, specials, limbs, least),
        in_specs=[SMEM] * 3,
        out_specs=[pl.BlockSpec(memory_space=pltpu.VMEM), SMEM, SMEM],
        out_shape=[
            jax.ShapeDtypeStruct((-(-PLAN * (most + 1) // (8 * LANES)) * 8, LANES), jnp.int32),
            jax.ShapeDtypeStruct((1,), jnp.int32),
            jax.ShapeDtypeStruct((count,), jnp.int32),
        ],
        scratch_shapes=[pltpu.VMEM((items, LANES), F32)] * 3,
        compiler_params=params(8),
        name="table",
    )(order, in_hbm(pos), spot)


def round_of(tile, t):
    got = [tile[lax.div(f, LANES), lax.rem(f, LANES)] for f in (jnp.asarray(PLAN * t + r, jnp.int32) for r in range(PLAN))]
    return got[:2], got[2:]


def pack_kernel(items, t, first, last, *refs):
    refs = list(refs)
    if t is None:
        t = refs.pop(0)[0]
    table, store = refs.pop(0), refs.pop(0)
    ins = () if first else (refs.pop(0), refs.pop(0))
    refs.pop(0)
    outs = () if last else (refs.pop(0), refs.pop(0))
    tile, keep, send, tsem = refs
    plan = pltpu.make_async_copy(table, tile, tsem)
    plan.start()
    plan.wait()
    go, came = round_of(tile, t)
    for i in range(len(ins)):
        @pl.when(came[i] < items)
        def _():
            pltpu.make_async_copy(ins[i], store.at[came[i]], keep.at[i]).start()

    old = []
    for j in range(len(outs)):
        fresh = [jnp.logical_and(go[j] == came[i], came[i] < items) for i in range(len(ins))]
        held = go[j] < items
        for f in fresh:
            held = jnp.logical_and(held, jnp.logical_not(f))
        old.append(held)

        @pl.when(held)
        def _():
            pltpu.make_async_copy(store.at[go[j]], outs[j], send.at[j]).start()

        for i in range(len(ins)):
            @pl.when(fresh[i])
            def _():
                outs[j][...] = ins[i][...]

    for i in range(len(ins)):
        @pl.when(came[i] < items)
        def _():
            pltpu.make_async_copy(ins[i], store.at[came[i]], keep.at[i]).wait()
    for j in range(len(outs)):
        @pl.when(old[j])
        def _():
            pltpu.make_async_copy(store.at[go[j]], outs[j], send.at[j]).wait()


def pack_call(table, t, store, ins=None, last=False):
    first = ins is None
    store = in_hbm(store)
    items = store.shape[0]
    item = jax.ShapeDtypeStruct(store.shape[1:], store.dtype)
    static = isinstance(t, int)
    args = (() if static else (t.reshape(1),)) + (table, store) + (() if first else tuple(ins))
    at = 1 if static else 2
    outs = [jax.ShapeDtypeStruct(store.shape, store.dtype)] + ([] if last else [item, item])
    size = math.prod(item.shape) * 4
    res = pl.pallas_call(
        functools.partial(pack_kernel, items, t if static else None, first, last),
        in_specs=([] if static else [SMEM]) + [ANY, HBM] + [VMEM] * (0 if first else 2),
        out_specs=[HBM] + [VMEM] * (len(outs) - 1),
        out_shape=outs,
        input_output_aliases={at: 0},
        scratch_shapes=[
            pltpu.SMEM(table.shape, jnp.int32),
            pltpu.SemaphoreType.DMA((2,)),
            pltpu.SemaphoreType.DMA((2,)),
            pltpu.SemaphoreType.DMA,
        ],
        compiler_params=params(2),
        cost_estimate=pl.CostEstimate(flops=0, bytes_accessed=8 * size, transcendentals=0),
        name="pack",
    )(*args)
    return res[0], list(res[1:])


def lower_kernel(low, high, guess, specials, limbs, *refs):
    tables, (diag, mats, *refs) = refs[:6], refs[6:]
    small, smem, refs = refs[-7:-1], refs[-1], refs[:-7]
    part, store, refs = refs[:2], refs[2:4], refs[4:]
    last = high is None
    scalars = [pltpu.make_async_copy(a, b, smem.at[i]) for i, (a, b) in enumerate(zip(tables, small))]
    order, digit, where, scale, conv, comp = small

    def fetch(k):
        return [
            pltpu.make_async_copy(store[c].at[pl.ds(k * specials, specials)], got.at[c], sem.at[c]) for c in range(2)
        ] + [pltpu.make_async_copy(diag.at[k], dg, sem.at[2])]

    if last:
        t, plan, *refs = refs
        ins, store, keep, send, refs = (refs[0:2], refs[2:4]), refs[4:6], refs[6:8], refs[8:10], refs[10:]
        total, got, dg, xs, sem, tile = refs
        total = [total.at[0], total.at[1]]
        copy = pltpu.make_async_copy(plan, tile, sem.at[7])
        copy.start()
    else:
        total, (got, dg, xs, sem) = refs[:2], refs[4:]
    scalars += [pltpu.make_async_copy(part[c], total[c], smem.at[len(small) + c]) for c in range(2)]
    for copy in fetch(guess) + scalars:
        copy.start()
    for copy in scalars + fetch(guess):
        copy.wait()
    count = diag.shape[0]
    first = where[0] * limbs

    if last:
        pltpu.make_async_copy(plan, tile, sem.at[7]).wait()
        _, came = round_of(tile, t[0])

        def arrive(act):
            for c in range(2):
                for i in range(2):
                    @pl.when(came[i] < store[c].shape[0])
                    def _():
                        act(pltpu.make_async_copy(ins[c][i], store[c].at[came[i]], sem.at[3 + 2 * c + i]))

        arrive(lambda copy: copy.start())
        for i in range(2):
            place = came[i] - guess * specials

            @pl.when(jnp.logical_and(place >= 0, place < specials))
            def _():
                for c in range(2):
                    got[c, place] = ins[c][i][...]

    def turn(i, carry):
        if last:
            @pl.when(i == 1)
            def _():
                arrive(lambda copy: copy.wait())

        k = lax.rem(guess + i, count)
        ripe = comp[k] > low
        if not last:
            ripe = jnp.logical_and(ripe, comp[k] <= high)

        @pl.when(ripe)
        def _():
            @pl.when(i > 0)
            def _():
                for copy in fetch(k):
                    copy.start()
                for copy in fetch(k):
                    copy.wait()

            def limb(m, carry):
                q = first + m

                @pl.when(digit[q] != DIGITS)
                def _():
                    h = (mats[m, 0], mats[m, 1])
                    w = [conv[q, order[DIGITS * specials + s]] for s in range(specials)]
                    size = scale[q]
                    step = 64
                    for c in range(2):
                        for i in range(2):
                            for r in range(0, RADIX, step):
                                x = w[0] * got[c, 0, pl.ds(i * RADIX + r, step), :]
                                for s in range(1, specials):
                                    x = x + w[s] * got[c, s, pl.ds(i * RADIX + r, step), :]
                                hi, lo = split(x)
                                xs[c, 0, pl.ds(r, step), pl.ds(i * LANES, LANES)] = hi
                                xs[c, 1, pl.ds(r, step), pl.ds(i * LANES, LANES)] = lo
                    for c in range(2):
                        y = mm(h, split(mm((xs[c, 0], xs[c, 1]), h)))
                        for i in range(2):
                            at = pl.ds(i * limbs + m, RADIX, stride=2 * limbs)
                            total[c][at, :] = total[c][at, :] - dg[at, :] * size * y[:, i * LANES : (i + 1) * LANES]

                return carry

            lax.fori_loop(0, limbs, limb, 0)

        return carry

    lax.fori_loop(0, count, turn, 0)
    if last:
        half = total[0].shape[0] // 2
        mine = where[1]
        for c in range(2):
            keep[c][...] = total[c][pl.ds(pl.multiple_of(mine * half, half), half), :]
            send[c][...] = total[c][pl.ds(pl.multiple_of((1 - mine) * half, half), half), :]


def lower_call(low, high, guess, order, digit, where, scale, conv, comp, diag, mats, specials, part, store, end=()):
    limbs = mats.shape[0]
    store = [in_hbm(s) for s in store]
    rows = part[0].shape[0]
    half = jax.ShapeDtypeStruct((rows // 2, LANES), F32)
    last = high is None
    part = part if last else [in_hbm(p) for p in part]
    shape = lambda a: jax.ShapeDtypeStruct(a.shape, a.dtype)
    scratch = [
        pltpu.VMEM((2, specials, 2 * RADIX, LANES), F32),
        pltpu.VMEM((rows, LANES), F32),
        pltpu.VMEM((2, 2, RADIX, RADIX), BF16),
        pltpu.SemaphoreType.DMA((8,)),
    ]
    if last:
        scratch = [pltpu.VMEM((2, rows, LANES), F32)] + scratch + [pltpu.SMEM(end[1].shape, jnp.int32)]
    tables = (order, in_hbm(digit), where, scale, in_hbm(conv), comp)
    scratch += [pltpu.SMEM(a.shape, a.dtype) for a in tables] + [pltpu.SemaphoreType.DMA((len(tables) + 2,))]
    return pl.pallas_call(
        functools.partial(lower_kernel, low, high, guess, specials, limbs),
        in_specs=[ANY] * 6 + [HBM, VMEM, ANY, ANY, HBM, HBM] + ([SMEM, ANY] + [VMEM] * 4 if last else []),
        out_specs=[HBM, HBM] + [VMEM] * 4 if last else [VMEM, VMEM, HBM, HBM],
        out_shape=[shape(s) for s in store] + [half] * 4 if last else [shape(p) for p in (*part, *store)],
        input_output_aliases={10: 0, 11: 1} if last else {10: 2, 11: 3},
        scratch_shapes=scratch,
        compiler_params=params(12),
        cost_estimate=pl.CostEstimate(flops=10**9, bytes_accessed=8 * 2**20, transcendentals=0),
        name="lower",
    )(*tables, in_hbm(diag), mats, *part, *store, *end)


def interleave(x):
    *lead, limbs, coeffs = x.shape
    x = x.reshape(*lead, limbs, coeffs // LANES, LANES)
    return jnp.swapaxes(x, -3, -2).reshape(*lead, coeffs // LANES * limbs, LANES)


def per_device(order_of, cipher, rotation_keys, diagonals, shifts, twiddles, moduli, digit_of, conversion):
    n = len(order_of)
    limbs = cipher.shape[0]
    ext = digit_of.shape[0]
    specials = ext // (DIGITS + 1)
    count = rotation_keys.shape[1]
    items = count * specials
    pos_of = np.argsort(np.array(order_of)).astype(np.int32)
    cw = [(order_of[i], order_of[(i + 1) % n]) for i in range(n)]
    ccw = [(b, a) for a, b in cw]
    me, rot = lax.axis_index("limb"), lax.axis_index("rot")
    where = jnp.stack([me, rot]).astype(jnp.int32)
    pos = jnp.asarray(pos_of)
    my_pos = pos[me]
    swap = lambda x: lax.ppermute(x, "rot", [(0, 1), (1, 0)])

    grid = np.arange(RADIX)
    angle = (grid[:, None] * grid[None, :] % RADIX) * (2.0 * math.pi / RADIX)
    base = ((np.cos(angle) + np.sin(angle)) / math.sqrt(RADIX)).astype(np.float32)
    base_hi = base.astype(BF16)
    base_lo = (base - base_hi.astype(np.float32)).astype(BF16)

    rows_c = interleave(cipher)
    keys = interleave(rotation_keys).reshape(count, DIGITS * 2, -1, LANES)
    diag = interleave(diagonals).reshape(count, -1, LANES)

    cut = limbs // 2
    given = (limbs, twiddles, where, jnp.asarray(base_hi), jnp.asarray(base_lo), rows_c)
    coef, mats = [None, None], None
    coef[0], mats = coef_call(0, cut, *given)
    coef[1], mats = coef_call(cut, limbs, *given, (mats,))

    ids = jnp.arange(ext, dtype=jnp.int32)
    before = (digit_of[None, :] < digit_of[:, None]) | (
        (digit_of[None, :] == digit_of[:, None]) & (ids[None, :] < ids[:, None])
    )
    place = jnp.sum(before.astype(jnp.int32), axis=1)
    order = jnp.sum(jnp.where(place[None, :] == ids[:, None], ids[None, :], 0), axis=1)
    slot = lax.dynamic_slice_in_dim(jnp.maximum(place - DIGITS * specials, -1), me * limbs, limbs, 0)
    special = digit_of == DIGITS
    mod = moduli.astype(F32)
    scale = jnp.sum(jnp.where(special[None, :], mod[:, None] / mod[None, :], 0.0), axis=1) / specials
    my_special = lax.dynamic_slice_in_dim(special, me * limbs, limbs, 0)
    my_gain = jnp.where(my_special, 1.0, lax.dynamic_slice_in_dim(scale, me * limbs, limbs, 0))
    rows8 = lambda v: jnp.broadcast_to(jnp.tile(v, 8 // limbs)[:, None], (8, LANES))
    gain = rows8(my_gain)
    fixed = items * n // (2 * n)
    plan, rounds, comp = table_call(n, count, specials, limbs, fixed, order, pos, my_pos.reshape(1))

    spans = [(0, cut), (cut, limbs)]
    blocks, lens, steps = list(coef), list(spans), [0, 0]
    right, left = list(coef), list(coef)
    hop = lambda x, ring: lax.ppermute(x, "limb", ring)
    both = (n - 1) // 2
    for r in range(1, both + 1):
        for i in range(2):
            right[i] = hop(right[i], cw)
            left[i] = hop(left[i], ccw)
        blocks += right + left
        lens += spans * 2
        steps += [-r, -r, r, r]
        if r == 2:
            right[1], left[1], order, slot, gain, scale, plan, rounds, comp = lax.optimization_barrier(
                (right[1], left[1], order, slot, gain, scale, plan, rounds, comp)
            )
    if n % 2 == 0:
        blocks += [hop(right[0], cw), hop(left[1], ccw)]
        lens += spans
        steps += [n // 2, n // 2]
    srcs = jnp.asarray(
        np.array([[order_of[(pos_of[d] + s) % n] for s in steps] for d in range(n)], np.int32)
    )[me]

    pad = 64
    mixed = mix_call(n, limbs, tuple(lens), order, digit_of, where, srcs, conversion, blocks)
    raised = raise_call(digit_of, where, mixed, swap(mixed), mats, rows_c, pad)

    def accumulate(k, after=None):
        return accum_call(k, tie(shifts, after), raised, keys, diag, gain, limbs, pad, part)

    def lower(low, high, guess, end=()):
        return lower_call(
            low, high, guess, order, digit_of, where, scale, conversion, comp, diag, mats, specials, part, stores, end
        )

    def tie(x, after):
        return x if after is None else lax.optimization_barrier((x, after))[0]

    def travel(sends):
        return [lax.ppermute(sends[0], "limb", cw), lax.ppermute(sends[1], "limb", ccw)]

    tasks = {max(2 * k - 3, 0): k for k in range(1, count)}, {max(2 * k - 2, 0): k for k in range(1, count)}
    gates = {fixed - 5: 0, fixed - 3: 1, fixed - 1: 2}
    part, stores, ins, low = None, None, [None, None], -1
    *part, acc = accumulate(0)
    stores = list(emit_call(0, slot, acc, mats, specials, items, stores))
    for t in range(fixed):
        for c in range(2):
            stores[c], sends = pack_call(plan, t, stores[c], ins[c])
            ins[c] = travel(sends)
        if t in tasks[0]:
            *part, acc = accumulate(tasks[0][t], sends[0])
            stores[0], acc = lax.optimization_barrier((stores[0], acc))
        if t in tasks[1]:
            stores = list(emit_call(tasks[1][t], slot, tie(acc, sends[0]), mats, specials, items, stores))
        if t in gates:
            *part, stores[0], stores[1] = lower(low, t, min(gates[t], count - 1))
            low = t

    def more(state):
        return state[0] < rounds[0]

    def one(state):
        t, stores, ins = state
        stores, ins = list(stores), list(ins)
        for c in range(2):
            stores[c], sends = pack_call(plan, t, stores[c], ins[c])
            ins[c] = travel(sends)
        return t + 1, stores, ins

    t, stores, ins = lax.while_loop(more, one, (jnp.int32(fixed), stores, ins))
    _, _, *halves = lower(low, None, count - 1, (t.reshape(1), plan, *ins[0], *ins[1]))
    total = jnp.stack([keep + swap(send) for keep, send in zip(halves[:2], halves[2:])])
    total = jnp.swapaxes(total.reshape(2, -1, limbs, LANES), 1, 2)
    return total.reshape(2, limbs, -1)


def solution(mesh):
    in_specs = (
        P(("parts", "limb"), None),
        P("rot", None, None, None, "limb", None),
        P("rot", None, "limb", None),
        P("rot", None),
        P(),
        P(),
        P(),
        P(),
    )
    out_specs = P(None, ("parts", "limb"), "rot")

    def step(*args):
        return per_device(ring_order(mesh), *args)

    return jax.shard_map(step, mesh=mesh, in_specs=in_specs, out_specs=out_specs, check_vma=False)
```

profile of v0, /device:TPU:0, one launch (start us, length us, event | category | flops | bytes accessed | tf_op | source)
XLA Modules:
  0.0 287.1 jit_solution(8261698512644453476)
XLA Ops:
  0.1 3.4 %coef.2 = (f32[2,256,128]{2,1,0:T(8,128)S(1)}, bf16[2,2,256,256]{3,2,1,0:T(8,128)(2,1)S(1)}) custom-call(s32[32]{0:T(128)} %tw.3, s32[2]{0:T(128)S(1)} %pad_add_fusion.where.refs_2_, bf16[256,256]{1,0:T(8,128)(2,1)} %constant.43.clone.base_hi, bf16[256,256]{1,0:T(8,128)(2,1)} %constant.44.clone.base_lo, f32[2048,128]{1,0:T(8,128)} %bitcast.45), custom_call_target="tpu_custom_call" | custom-call | flops 1000000000 | bytes 1048576 | tf_op jit(solution)/shard_map/coef/pallas_call | solution.py:109
  3.5 3.4 %coef.3 = (f32[2,256,128]{2,1,0:T(8,128)S(1)}, bf16[4,2,256,256]{3,2,1,0:T(8,128)(2,1)S(1)}) custom-call(s32[32]{0:T(128)} %tw.3, s32[2]{0:T(128)S(1)} %pad_add_fusion.where.refs_2_, bf16[256,256]{1,0:T(8,128)(2,1)} %constant.43.clone.base_hi, bf16[256,256]{1,0:T(8,128)(2,1)} %constant.44.clone.base_lo, f32[2048,128]{1,0:T(8,128)} %bitcast.46, ...), custom_call_target="tpu_custom_call" | custom-call | flops 1000000000 | bytes 1048576 | tf_op jit(solution)/shard_map/coef/pallas_call | solution.py:109
  6.9 3.0 %collective-permute-start.4 = (f32[2,256,128]{2,1,0:T(8,128)S(1)}, f32[2,256,128]{2,1,0:T(8,128)S(1)}, u32[]{:S(2)}, u32[]{:S(2)}) collective-permute-start(f32[2,256,128]{2,1,0:T(8,128)S(1)} %get-tuple-element.226.refs_1_), channel_id=1, source_target_pairs={{0,2},{2,6},{6,10},{10,14},{14,12},{12,8},{8,4},{4,0},{1,3},{3,7},... | collective-permute-start | bytes 786440 | tf_op jit(solution)/shard_map/ppermute | solution.py:726
  10.1 1.9 collective-permute-start.8
  14.7 2.5 collective-permute-done.4.refs_3_
  17.1 2.0 collective-permute-start.5
  19.2 3.5 %collective-permute-done.8.refs_2_ = f32[2,256,128]{2,1,0:T(8,128)S(1)} collective-permute-done((f32[2,256,128]{2,1,0:T(8,128)S(1)}, f32[2,256,128]{2,1,0:T(8,128)S(1)}, u32[]{:S(2)}, u32[]{:S(2)}) %collective-permute-start.8) | collective-permute-done | bytes 262176 | tf_op jit(solution)/shard_map/ppermute | solution.py:726
  22.8 2.0 collective-permute-start.10
  26.2 5.7 %table.1 = (s32[8,128]{1,0:T(8,128)S(1)}, s32[1]{0:T(128)}, s32[4]{0:T(128)S(1)}) custom-call(s32[32]{0:T(128)S(1)} %select_reduce_fusion.order.refs_0_, s32[8]{0:T(128)} %constant.42.clone.pos, s32[1]{0:T(128)} %dynamic_slice.18.spot), custom_call_target="tpu_custom_call" | custom-call | tf_op jit(solution)/shard_map/table/pallas_call | solution.py:434
  32.0 2.0 collective-permute-start.15
  36.4 4.6 %collective-permute-done.11.refs_8_ = f32[2,256,128]{2,1,0:T(8,128)S(1)} collective-permute-done((f32[2,256,128]{2,1,0:T(8,128)S(1)}, f32[2,256,128]{2,1,0:T(8,128)S(1)}, u32[]{:S(2)}, u32[]{:S(2)}) %collective-permute-start.11) | collective-permute-done | bytes 262176 | tf_op jit(solution)/shard_map/ppermute | solution.py:726
  41.1 5.5 %collective-permute-done.15.refs_13_ = f32[2,256,128]{2,1,0:T(8,128)S(1)} collective-permute-done((f32[2,256,128]{2,1,0:T(8,128)S(1)}, f32[2,256,128]{2,1,0:T(8,128)S(1)}, u32[]{:S(2)}, u32[]{:S(2)}) %collective-permute-start.15) | collective-permute-done | bytes 262176 | tf_op jit(solution)/shard_map/ppermute | solution.py:726
  46.8 2.0 collective-permute-start.16
  49.4 2.3 collective-permute-done.14.refs_12_
  51.7 2.8 collective-permute-done.17.refs_15_
  54.5 2.8 mix.1.own
  57.4 3.4 %collective-permute-done.18.other = f32[3,4,256,128]{3,2,1,0:T(8,128)S(1)} collective-permute-done((f32[3,4,256,128]{3,2,1,0:T(8,128)S(1)}, f32[3,4,256,128]{3,2,1,0:T(8,128)S(1)}, u32[]{:S(2)}, u32[]{:S(2)}) %collective-permute-start.18) | collective-permute-done | bytes 1572896 | tf_op jit(solution)/shard_map/ppermute | solution.py:688
  60.8 5.5 %raise.1.raised = f32[4,2112,128]{2,1,0:T(8,128)S(1)} custom-call(s32[32]{0:T(128)} %refs_1_.7, s32[2]{0:T(128)S(1)} %pad_add_fusion.where.refs_2_, f32[3,4,256,128]{3,2,1,0:T(8,128)S(1)} %mix.1.own, f32[3,4,256,128]{3,2,1,0:T(8,128)S(1)} %collective-permute-done.18.other, bf16[4,2,256,256]{3,2,1,0:T(8,128)(2,1)S(1)} %get-tuple-element.233.mats.refs_7_, ...), custom_call_target="tpu_custom_call" | custom-call | tf_op jit(solution)/shard_map/raise/pallas_call | solution.py:222
  66.3 3.7 %accum.4 = (f32[2048,128]{1,0:T(8,128)S(1)}, f32[2048,128]{1,0:T(8,128)S(1)}, f32[2,2048,128]{2,1,0:T(8,128)S(1)}) custom-call(s32[1,4]{1,0:T(1,128)} %shifts.4, f32[4,2112,128]{2,1,0:T(8,128)S(1)} %raise.1.raised, f32[4,6,2048,128]{3,2,1,0:T(8,128)} %bitcast.31, f32[4,2048,128]{2,1,0:T(8,128)} %bitcast.35, f32[8,128]{1,0:T(8,128)S(1)} %broadcast_in_dim.50.gain), custom_call_target="tpu_custom_call" | custom-call | flops 100000000 | bytes 8388608 | tf_op jit(solution)/shard_map/accum/pallas_call | solution.py:295
  70.1 3.7 %emit.4 = (f32[32,512,128]{2,1,0:T(8,128)}, f32[32,512,128]{2,1,0:T(8,128)}) custom-call(s32[4]{0:T(128)S(1)} %dynamic_slice.15.slot, f32[2,2048,128]{2,1,0:T(8,128)S(1)} %get-tuple-element.240.acc, bf16[4,2,256,256]{3,2,1,0:T(8,128)(2,1)S(1)} %get-tuple-element.233.mats.refs_7_), custom_call_target="tpu_custom_call" | custom-call | flops 1000000000 | bytes 1048576 | tf_op jit(solution)/shard_map/emit/pallas_call | solution.py:343
  75.7 1.9 collective-permute-start.22
  79.4 1.9 collective-permute-start.20
  81.3 3.8 %accum.5 = (f32[2048,128]{1,0:T(8,128)S(1)}, f32[2048,128]{1,0:T(8,128)S(1)}, f32[2,2048,128]{2,1,0:T(8,128)S(1)}) custom-call(s32[1,4]{1,0:T(1,128)} %shifts.4, f32[4,2112,128]{2,1,0:T(8,128)S(1)} %raise.1.raised, f32[4,6,2048,128]{3,2,1,0:T(8,128)} %bitcast.32, f32[4,2048,128]{2,1,0:T(8,128)} %bitcast.36, ...), custom_call_target="tpu_custom_call", output_to_operand_aliasing={{0}: (5, {}), {1}: (6, {})} | custom-call | flops 100000000 | bytes 8388608 | tf_op jit(solution)/shard_map/accum/pallas_call | solution.py:295
  85.1 3.8 %emit.5 = (f32[32,512,128]{2,1,0:T(8,128)}, f32[32,512,128]{2,1,0:T(8,128)}) custom-call(s32[4]{0:T(128)S(1)} %dynamic_slice.15.slot, f32[2,2048,128]{2,1,0:T(8,128)S(1)} %get-tuple-element.250.acc, bf16[4,2,256,256]{3,2,1,0:T(8,128)(2,1)S(1)} %get-tuple-element.233.mats.refs_7_, ...), custom_call_target="tpu_custom_call", output_to_operand_aliasing={{0}: (3, {}), {1}: (4, {})} | custom-call | flops 1000000000 | bytes 1048576 | tf_op jit(solution)/shard_map/emit/pallas_call | solution.py:343
  90.8 2.0 collective-permute-start.24
  94.6 2.0 collective-permute-start.26
  96.7 3.8 %accum.6 = (f32[2048,128]{1,0:T(8,128)S(1)}, f32[2048,128]{1,0:T(8,128)S(1)}, f32[2,2048,128]{2,1,0:T(8,128)S(1)}) custom-call(s32[1,4]{1,0:T(1,128)} %shifts.4, f32[4,2112,128]{2,1,0:T(8,128)S(1)} %raise.1.raised, f32[4,6,2048,128]{3,2,1,0:T(8,128)} %bitcast.33, f32[4,2048,128]{2,1,0:T(8,128)} %bitcast.37, ...), custom_call_target="tpu_custom_call", output_to_operand_aliasing={{0}: (5, {}), {1}: (6, {})} | custom-call | flops 100000000 | bytes 8388608 | tf_op jit(solution)/shard_map/accum/pallas_call | solution.py:295
  100.5 1.9 pack.38
  102.4 2.0 collective-permute-start.27
  104.4 1.9 pack.39
  106.3 2.5 collective-permute-start.29
  108.8 3.8 %emit.6 = (f32[32,512,128]{2,1,0:T(8,128)}, f32[32,512,128]{2,1,0:T(8,128)}) custom-call(s32[4]{0:T(128)S(1)} %dynamic_slice.15.slot, f32[2,2048,128]{2,1,0:T(8,128)S(1)} %get-tuple-element.268.acc, bf16[4,2,256,256]{3,2,1,0:T(8,128)(2,1)S(1)} %get-tuple-element.233.mats.refs_7_, ...), custom_call_target="tpu_custom_call", output_to_operand_aliasing={{0}: (3, {}), {1}: (4, {})} | custom-call | flops 1000000000 | bytes 1048576 | tf_op jit(solution)/shard_map/emit/pallas_call | solution.py:343
  113.0 1.9 pack.40
  114.9 2.3 collective-permute-start.31
  118.5 1.9 pack.41
  122.4 3.8 %accum.7 = (f32[2048,128]{1,0:T(8,128)S(1)}, f32[2048,128]{1,0:T(8,128)S(1)}, f32[2,2048,128]{2,1,0:T(8,128)S(1)}) custom-call(s32[1,4]{1,0:T(1,128)} %shifts.4, f32[4,2112,128]{2,1,0:T(8,128)S(1)} %raise.1.raised, f32[4,6,2048,128]{3,2,1,0:T(8,128)} %bitcast.34, f32[4,2048,128]{2,1,0:T(8,128)} %bitcast.38, ...), custom_call_target="tpu_custom_call", output_to_operand_aliasing={{0}: (5, {}), {1}: (6, {})} | custom-call | flops 100000000 | bytes 8388608 | tf_op jit(solution)/shard_map/accum/pallas_call | solution.py:295
  126.3 1.9 pack.42
  130.3 1.9 pack.43
  134.3 3.7 %emit.7 = (f32[32,512,128]{2,1,0:T(8,128)}, f32[32,512,128]{2,1,0:T(8,128)}) custom-call(s32[4]{0:T(128)S(1)} %dynamic_slice.15.slot, f32[2,2048,128]{2,1,0:T(8,128)S(1)} %get-tuple-element.291.acc, bf16[4,2,256,256]{3,2,1,0:T(8,128)(2,1)S(1)} %get-tuple-element.233.mats.refs_7_, ...), custom_call_target="tpu_custom_call", output_to_operand_aliasing={{0}: (3, {}), {1}: (4, {})} | custom-call | flops 1000000000 | bytes 1048576 | tf_op jit(solution)/shard_map/emit/pallas_call | solution.py:343
  138.0 1.9 pack.51
  140.0 2.0 collective-permute-start.52
  142.9 1.9 pack.44
  145.1 1.8 collective-permute-start.38
  148.6 1.9 pack.52
  154.2 1.9 pack.45
  160.2 1.9 pack.53
  166.1 1.9 pack.46
  170.7 1.9 collective-permute-done.56.refs_3_
  172.6 1.9 pack.54
  178.6 1.9 pack.47
  184.2 1.9 pack.55
  189.8 1.9 pack.48
  216.4 5.6 %lower.4 = (f32[2048,128]{1,0:T(8,128)S(1)}, f32[2048,128]{1,0:T(8,128)S(1)}, f32[32,512,128]{2,1,0:T(8,128)}, f32[32,512,128]{2,1,0:T(8,128)}) custom-call(s32[32]{0:T(128)S(1)} %select_reduce_fusion.order.refs_0_, s32[32]{0:T(128)} %refs_1_.7, s32[2]{0:T(128)S(1)} %pad_add_fusion.where.refs_2_, ...), custom_call_target="tpu_custom_call", output_to_operand_aliasing={{2}: (10, {}), {3}: (11, {})} | custom-call | flops 1000000000 | bytes 8388608 | tf_op jit(solution)/shard_map/lower/pallas_call | solution.py:655
  222.1 1.9 pack.60
  226.8 1.9 pack.58
  230.8 3.1 %collective-permute-done.69.refs_2_ = f32[512,128]{1,0:T(8,128)S(1)} collective-permute-done((f32[512,128]{1,0:T(8,128)S(1)}, f32[512,128]{1,0:T(8,128)S(1)}, u32[]{:S(2)}, u32[]{:S(2)}) %collective-permute-start.69) | collective-permute-done | bytes 262176 | tf_op jit(solution)/shard_map/ppermute | solution.py:763
  241.6 1.8 collective-permute-start.72
  243.4 5.6 %lower.5 = (f32[2048,128]{1,0:T(8,128)S(1)}, f32[2048,128]{1,0:T(8,128)S(1)}, f32[32,512,128]{2,1,0:T(8,128)}, f32[32,512,128]{2,1,0:T(8,128)}) custom-call(s32[32]{0:T(128)S(1)} %select_reduce_fusion.order.refs_0_, s32[32]{0:T(128)} %refs_1_.7, s32[2]{0:T(128)S(1)} %pad_add_fusion.where.refs_2_, ...), custom_call_target="tpu_custom_call", output_to_operand_aliasing={{2}: (10, {}), {3}: (11, {})} | custom-call | flops 1000000000 | bytes 8388608 | tf_op jit(solution)/shard_map/lower/pallas_call | solution.py:655
  259.9 2.1 pack.65
  262.0 2.7 collective-permute-start.81
  264.7 2.2 pack.63
  266.9 2.3 collective-permute-start.79
  269.3 5.6 %lower.6 = (f32[2048,128]{1,0:T(8,128)S(1)}, f32[2048,128]{1,0:T(8,128)S(1)}, f32[32,512,128]{2,1,0:T(8,128)}, f32[32,512,128]{2,1,0:T(8,128)}) custom-call(s32[32]{0:T(128)S(1)} %select_reduce_fusion.order.refs_0_, s32[32]{0:T(128)} %refs_1_.7, s32[2]{0:T(128)S(1)} %pad_add_fusion.where.refs_2_, ...), custom_call_target="tpu_custom_call", output_to_operand_aliasing={{2}: (10, {}), {3}: (11, {})} | custom-call | flops 1000000000 | bytes 8388608 | tf_op jit(solution)/shard_map/lower/pallas_call | solution.py:655
  276.7 6.4 %lower.7 = (f32[32,512,128]{2,1,0:T(8,128)}, f32[32,512,128]{2,1,0:T(8,128)}, f32[1024,128]{1,0:T(8,128)S(1)}, f32[1024,128]{1,0:T(8,128)S(1)}, f32[1024,128]{1,0:T(8,128)S(1)}, /*index=5*/f32[1024,128]{1,0:T(8,128)S(1)}) custom-call(s32[32]{0:T(128)S(1)} %select_reduce_fusion.order.refs_0_, ...), custom_call_target="tpu_custom_call", output_to_operand_aliasing={{0}: (10, {}), {1}: (11, {})} | custom-call | flops 1000000000 | bytes 8388608 | tf_op jit(solution)/shard_map/lower/pallas_call | solution.py:655
  (178 shorter events, 106.4 us)
Async XLA Ops:
  6.9 10.3 %collective-permute-start.4 = (f32[2,256,128]{2,1,0:T(8,128)S(1)}, f32[2,256,128]{2,1,0:T(8,128)S(1)}, u32[]{:S(2)}, u32[]{:S(2)}) collective-permute-start(f32[2,256,128]{2,1,0:T(8,128)S(1)} %get-tuple-element.226.refs_1_), channel_id=1, source_target_pairs={{0,2},{2,6},{6,10},{10,14},{14,12},{12,8},{8,4},{4,0},{1,3},{3,7},... | collective-permute-start | bytes 786440 | tf_op jit(solution)/shard_map/ppermute | solution.py:726
  9.9 9.2 %collective-permute-start.6 = (f32[2,256,128]{2,1,0:T(8,128)S(1)}, f32[2,256,128]{2,1,0:T(8,128)S(1)}, u32[]{:S(2)}, u32[]{:S(2)}) collective-permute-start(f32[2,256,128]{2,1,0:T(8,128)S(1)} %get-tuple-element.226.refs_1_), channel_id=1, source_target_pairs={{2,0},{6,2},{10,6},{14,10},{12,14},{8,12},{4,8},{0,4},{3,1},{7,3},... | collective-permute-start | bytes 786440 | tf_op jit(solution)/shard_map/ppermute | solution.py:726
  10.1 12.7 %collective-permute-start.8 = (f32[2,256,128]{2,1,0:T(8,128)S(1)}, f32[2,256,128]{2,1,0:T(8,128)S(1)}, u32[]{:S(2)}, u32[]{:S(2)}) collective-permute-start(f32[2,256,128]{2,1,0:T(8,128)S(1)} %get-tuple-element.236.refs_0_), channel_id=1, source_target_pairs={{0,2},{2,6},{6,10},{10,14},{14,12},{12,8},{8,4},{4,0},{1,3},{3,7},... | collective-permute-start | bytes 786440 | tf_op jit(solution)/shard_map/ppermute | solution.py:726
  12.0 19.9 %collective-permute-start.9 = (f32[2,256,128]{2,1,0:T(8,128)S(1)}, f32[2,256,128]{2,1,0:T(8,128)S(1)}, u32[]{:S(2)}, u32[]{:S(2)}) collective-permute-start(f32[2,256,128]{2,1,0:T(8,128)S(1)} %get-tuple-element.236.refs_0_), channel_id=1, source_target_pairs={{2,0},{6,2},{10,6},{14,10},{12,14},{8,12},{4,8},{0,4},{3,1},{7,3},... | collective-permute-start | bytes 786440 | tf_op jit(solution)/shard_map/ppermute | solution.py:726
  17.1 14.8 %collective-permute-start.5 = (f32[2,256,128]{2,1,0:T(8,128)S(1)}, f32[2,256,128]{2,1,0:T(8,128)S(1)}, u32[]{:S(2)}, u32[]{:S(2)}) collective-permute-start(f32[2,256,128]{2,1,0:T(8,128)S(1)} %collective-permute-done.4.refs_3_), channel_id=1, source_target_pairs={{0,2},{2,6},{6,10},{10,14},{14,12},{12,8},{8,4},{4,0},{1,3},{3,7},... | collective-permute-start | bytes 786440 | tf_op jit(solution)/shard_map/ppermute | solution.py:726
  19.1 12.9 %collective-permute-start.7 = (f32[2,256,128]{2,1,0:T(8,128)S(1)}, f32[2,256,128]{2,1,0:T(8,128)S(1)}, u32[]{:S(2)}, u32[]{:S(2)}) collective-permute-start(f32[2,256,128]{2,1,0:T(8,128)S(1)} %collective-permute-done.6.refs_5_), channel_id=1, source_target_pairs={{2,0},{6,2},{10,6},{14,10},{12,14},{8,12},{4,8},{0,4},{3,1},{7,3},... | collective-permute-start | bytes 786440 | tf_op jit(solution)/shard_map/ppermute | solution.py:726
  22.8 11.3 %collective-permute-start.10 = (f32[2,256,128]{2,1,0:T(8,128)S(1)}, f32[2,256,128]{2,1,0:T(8,128)S(1)}, u32[]{:S(2)}, u32[]{:S(2)}) collective-permute-start(f32[2,256,128]{2,1,0:T(8,128)S(1)} %collective-permute-done.8.refs_2_), channel_id=1, source_target_pairs={{0,2},{2,6},{6,10},{10,14},{14,12},{12,8},{8,4},{4,0},{1,3},{3,7},... | collective-permute-start | bytes 786440 | tf_op jit(solution)/shard_map/ppermute | solution.py:726
  31.8 9.2 %collective-permute-start.11 = (f32[2,256,128]{2,1,0:T(8,128)S(1)}, f32[2,256,128]{2,1,0:T(8,128)S(1)}, u32[]{:S(2)}, u32[]{:S(2)}) collective-permute-start(f32[2,256,128]{2,1,0:T(8,128)S(1)} %collective-permute-done.9.refs_4_), channel_id=1, source_target_pairs={{2,0},{6,2},{10,6},{14,10},{12,14},{8,12},{4,8},{0,4},{3,1},{7,3},... | collective-permute-start | bytes 786440 | tf_op jit(solution)/shard_map/ppermute | solution.py:726
  32.0 14.7 %collective-permute-start.15 = (f32[2,256,128]{2,1,0:T(8,128)S(1)}, f32[2,256,128]{2,1,0:T(8,128)S(1)}, u32[]{:S(2)}, u32[]{:S(2)}) collective-permute-start(f32[2,256,128]{2,1,0:T(8,128)S(1)} %collective-permute-done.7.refs_9_), channel_id=1, source_target_pairs={{2,0},{6,2},{10,6},{14,10},{12,14},{8,12},{4,8},{0,4},{3,1},{7,3},... | collective-permute-start | bytes 786440 | tf_op jit(solution)/shard_map/ppermute | solution.py:726
  34.1 12.7 %collective-permute-start.12 = (f32[2,256,128]{2,1,0:T(8,128)S(1)}, f32[2,256,128]{2,1,0:T(8,128)S(1)}, u32[]{:S(2)}, u32[]{:S(2)}) collective-permute-start(f32[2,256,128]{2,1,0:T(8,128)S(1)} %collective-permute-done.10.refs_6_), channel_id=1, source_target_pairs={{0,2},{2,6},{6,10},{10,14},{14,12},{12,8},{8,4},{4,0},{1,3},{3,7},... | collective-permute-start | bytes 786440 | tf_op jit(solution)/shard_map/ppermute | solution.py:726
  34.8 14.6 %collective-permute-start.13 = (f32[2,256,128]{2,1,0:T(8,128)S(1)}, f32[2,256,128]{2,1,0:T(8,128)S(1)}, u32[]{:S(2)}, u32[]{:S(2)}) collective-permute-start(f32[2,256,128]{2,1,0:T(8,128)S(1)} %collective-permute-done.5.refs_7_), channel_id=1, source_target_pairs={{0,2},{2,6},{6,10},{10,14},{14,12},{12,8},{8,4},{4,0},{1,3},{3,7},... | collective-permute-start | bytes 786440 | tf_op jit(solution)/shard_map/ppermute | solution.py:726
  41.1 10.6 %collective-permute-start.14 = (f32[2,256,128]{2,1,0:T(8,128)S(1)}, f32[2,256,128]{2,1,0:T(8,128)S(1)}, u32[]{:S(2)}, u32[]{:S(2)}) collective-permute-start(f32[2,256,128]{2,1,0:T(8,128)S(1)} %collective-permute-done.11.refs_8_), channel_id=1, source_target_pairs={{2,0},{6,2},{10,6},{14,10},{12,14},{8,12},{4,8},{0,4},{3,1},{7,3},... | collective-permute-start | bytes 786440 | tf_op jit(solution)/shard_map/ppermute | solution.py:726
  75.5 13.4 %collective-permute-start.21 = (f32[512,128]{1,0:T(8,128)S(1)}, f32[512,128]{1,0:T(8,128)S(1)}, u32[]{:S(2)}, u32[]{:S(2)}) collective-permute-start(f32[512,128]{1,0:T(8,128)S(1)} %get-tuple-element.244), channel_id=1, source_target_pairs={{0,2},{2,6},{6,10},{10,14},{14,12},{12,8},{8,4},{4,0},{1,3},{3,7},... | collective-permute-start | bytes 786440 | tf_op jit(solution)/shard_map/ppermute | solution.py:763
  75.7 13.3 %collective-permute-start.22 = (f32[512,128]{1,0:T(8,128)S(1)}, f32[512,128]{1,0:T(8,128)S(1)}, u32[]{:S(2)}, u32[]{:S(2)}) collective-permute-start(f32[512,128]{1,0:T(8,128)S(1)} %get-tuple-element.258), channel_id=1, source_target_pairs={{2,0},{6,2},{10,6},{14,10},{12,14},{8,12},{4,8},{0,4},{3,1},{7,3},... | collective-permute-start | bytes 786440 | tf_op jit(solution)/shard_map/ppermute | solution.py:763
  79.2 13.6 %collective-permute-start.19 = (f32[512,128]{1,0:T(8,128)S(1)}, f32[512,128]{1,0:T(8,128)S(1)}, u32[]{:S(2)}, u32[]{:S(2)}) collective-permute-start(f32[512,128]{1,0:T(8,128)S(1)} %get-tuple-element.254), channel_id=1, source_target_pairs={{0,2},{2,6},{6,10},{10,14},{14,12},{12,8},{8,4},{4,0},{1,3},{3,7},... | collective-permute-start | bytes 786440 | tf_op jit(solution)/shard_map/ppermute | solution.py:763
  79.4 13.4 %collective-permute-start.20 = (f32[512,128]{1,0:T(8,128)S(1)}, f32[512,128]{1,0:T(8,128)S(1)}, u32[]{:S(2)}, u32[]{:S(2)}) collective-permute-start(f32[512,128]{1,0:T(8,128)S(1)} %get-tuple-element.255), channel_id=1, source_target_pairs={{2,0},{6,2},{10,6},{14,10},{12,14},{8,12},{4,8},{0,4},{3,1},{7,3},... | collective-permute-start | bytes 786440 | tf_op jit(solution)/shard_map/ppermute | solution.py:763
  90.7 9.8 %collective-permute-start.23 = (f32[512,128]{1,0:T(8,128)S(1)}, f32[512,128]{1,0:T(8,128)S(1)}, u32[]{:S(2)}, u32[]{:S(2)}) collective-permute-start(f32[512,128]{1,0:T(8,128)S(1)} %get-tuple-element.259), channel_id=1, source_target_pairs={{0,2},{2,6},{6,10},{10,14},{14,12},{12,8},{8,4},{4,0},{1,3},{3,7},... | collective-permute-start | bytes 786440 | tf_op jit(solution)/shard_map/ppermute | solution.py:763
  90.8 9.7 %collective-permute-start.24 = (f32[512,128]{1,0:T(8,128)S(1)}, f32[512,128]{1,0:T(8,128)S(1)}, u32[]{:S(2)}, u32[]{:S(2)}) collective-permute-start(f32[512,128]{1,0:T(8,128)S(1)} %get-tuple-element.266), channel_id=1, source_target_pairs={{2,0},{6,2},{10,6},{14,10},{12,14},{8,12},{4,8},{0,4},{3,1},{7,3},... | collective-permute-start | bytes 786440 | tf_op jit(solution)/shard_map/ppermute | solution.py:763
  94.6 9.9 %collective-permute-start.25 = (f32[512,128]{1,0:T(8,128)S(1)}, f32[512,128]{1,0:T(8,128)S(1)}, u32[]{:S(2)}, u32[]{:S(2)}) collective-permute-start(f32[512,128]{1,0:T(8,128)S(1)} %get-tuple-element.270), channel_id=1, source_target_pairs={{0,2},{2,6},{6,10},{10,14},{14,12},{12,8},{8,4},{4,0},{1,3},{3,7},... | collective-permute-start | bytes 786440 | tf_op jit(solution)/shard_map/ppermute | solution.py:763
  94.6 9.8 %collective-permute-start.26 = (f32[512,128]{1,0:T(8,128)S(1)}, f32[512,128]{1,0:T(8,128)S(1)}, u32[]{:S(2)}, u32[]{:S(2)}) collective-permute-start(f32[512,128]{1,0:T(8,128)S(1)} %get-tuple-element.271), channel_id=1, source_target_pairs={{2,0},{6,2},{10,6},{14,10},{12,14},{8,12},{4,8},{0,4},{3,1},{7,3},... | collective-permute-start | bytes 786440 | tf_op jit(solution)/shard_map/ppermute | solution.py:763
  102.4 10.2 %collective-permute-start.27 = (f32[512,128]{1,0:T(8,128)S(1)}, f32[512,128]{1,0:T(8,128)S(1)}, u32[]{:S(2)}, u32[]{:S(2)}) collective-permute-start(f32[512,128]{1,0:T(8,128)S(1)} %get-tuple-element.267), channel_id=1, source_target_pairs={{0,2},{2,6},{6,10},{10,14},{14,12},{12,8},{8,4},{4,0},{1,3},{3,7},... | collective-permute-start | bytes 786440 | tf_op jit(solution)/shard_map/ppermute | solution.py:763
  106.3 10.8 %collective-permute-start.29 = (f32[512,128]{1,0:T(8,128)S(1)}, f32[512,128]{1,0:T(8,128)S(1)}, u32[]{:S(2)}, u32[]{:S(2)}) collective-permute-start(f32[512,128]{1,0:T(8,128)S(1)} %get-tuple-element.283), channel_id=1, source_target_pairs={{0,2},{2,6},{6,10},{10,14},{14,12},{12,8},{8,4},{4,0},{1,3},{3,7},... | collective-permute-start | bytes 786440 | tf_op jit(solution)/shard_map/ppermute | solution.py:763
  108.8 9.7 %collective-permute-start.30 = (f32[512,128]{1,0:T(8,128)S(1)}, f32[512,128]{1,0:T(8,128)S(1)}, u32[]{:S(2)}, u32[]{:S(2)}) collective-permute-start(f32[512,128]{1,0:T(8,128)S(1)} %get-tuple-element.284), channel_id=1, source_target_pairs={{2,0},{6,2},{10,6},{14,10},{12,14},{8,12},{4,8},{0,4},{3,1},{7,3},... | collective-permute-start | bytes 786440 | tf_op jit(solution)/shard_map/ppermute | solution.py:763
  114.9 11.4 %collective-permute-start.31 = (f32[512,128]{1,0:T(8,128)S(1)}, f32[512,128]{1,0:T(8,128)S(1)}, u32[]{:S(2)}, u32[]{:S(2)}) collective-permute-start(f32[512,128]{1,0:T(8,128)S(1)} %get-tuple-element.276), channel_id=1, source_target_pairs={{0,2},{2,6},{6,10},{10,14},{14,12},{12,8},{8,4},{4,0},{1,3},{3,7},... | collective-permute-start | bytes 786440 | tf_op jit(solution)/shard_map/ppermute | solution.py:763
  117.1 9.1 %collective-permute-start.32 = (f32[512,128]{1,0:T(8,128)S(1)}, f32[512,128]{1,0:T(8,128)S(1)}, u32[]{:S(2)}, u32[]{:S(2)}) collective-permute-start(f32[512,128]{1,0:T(8,128)S(1)} %get-tuple-element.289), channel_id=1, source_target_pairs={{2,0},{6,2},{10,6},{14,10},{12,14},{8,12},{4,8},{0,4},{3,1},{7,3},... | collective-permute-start | bytes 786440 | tf_op jit(solution)/shard_map/ppermute | solution.py:763
  120.3 10.0 %collective-permute-start.33 = (f32[512,128]{1,0:T(8,128)S(1)}, f32[512,128]{1,0:T(8,128)S(1)}, u32[]{:S(2)}, u32[]{:S(2)}) collective-permute-start(f32[512,128]{1,0:T(8,128)S(1)} %get-tuple-element.293), channel_id=1, source_target_pairs={{0,2},{2,6},{6,10},{10,14},{14,12},{12,8},{8,4},{4,0},{1,3},{3,7},... | collective-permute-start | bytes 786440 | tf_op jit(solution)/shard_map/ppermute | solution.py:763
  128.2 9.8 %collective-permute-start.49 = (f32[512,128]{1,0:T(8,128)S(1)}, f32[512,128]{1,0:T(8,128)S(1)}, u32[]{:S(2)}, u32[]{:S(2)}) collective-permute-start(f32[512,128]{1,0:T(8,128)S(1)} %get-tuple-element.290), channel_id=1, source_target_pairs={{0,2},{2,6},{6,10},{10,14},{14,12},{12,8},{8,4},{4,0},{1,3},{3,7},... | collective-permute-start | bytes 786440 | tf_op jit(solution)/shard_map/ppermute | solution.py:763
  132.2 9.8 %collective-permute-start.35 = (f32[512,128]{1,0:T(8,128)S(1)}, f32[512,128]{1,0:T(8,128)S(1)}, u32[]{:S(2)}, u32[]{:S(2)}) collective-permute-start(f32[512,128]{1,0:T(8,128)S(1)} %get-tuple-element.298), channel_id=1, source_target_pairs={{0,2},{2,6},{6,10},{10,14},{14,12},{12,8},{8,4},{4,0},{1,3},{3,7},... | collective-permute-start | bytes 786440 | tf_op jit(solution)/shard_map/ppermute | solution.py:763
  133.7 9.2 %collective-permute-start.36 = (f32[512,128]{1,0:T(8,128)S(1)}, f32[512,128]{1,0:T(8,128)S(1)}, u32[]{:S(2)}, u32[]{:S(2)}) collective-permute-start(f32[512,128]{1,0:T(8,128)S(1)} %get-tuple-element.299), channel_id=1, source_target_pairs={{2,0},{6,2},{10,6},{14,10},{12,14},{8,12},{4,8},{0,4},{3,1},{7,3},... | collective-permute-start | bytes 786440 | tf_op jit(solution)/shard_map/ppermute | solution.py:763
  144.8 9.0 %collective-permute-start.37 = (f32[512,128]{1,0:T(8,128)S(1)}, f32[512,128]{1,0:T(8,128)S(1)}, u32[]{:S(2)}, u32[]{:S(2)}) collective-permute-start(f32[512,128]{1,0:T(8,128)S(1)} %get-tuple-element.301), channel_id=1, source_target_pairs={{0,2},{2,6},{6,10},{10,14},{14,12},{12,8},{8,4},{4,0},{1,3},{3,7},... | collective-permute-start | bytes 786440 | tf_op jit(solution)/shard_map/ppermute | solution.py:763
  145.1 9.2 %collective-permute-start.38 = (f32[512,128]{1,0:T(8,128)S(1)}, f32[512,128]{1,0:T(8,128)S(1)}, u32[]{:S(2)}, u32[]{:S(2)}) collective-permute-start(f32[512,128]{1,0:T(8,128)S(1)} %get-tuple-element.302), channel_id=1, source_target_pairs={{2,0},{6,2},{10,6},{14,10},{12,14},{8,12},{4,8},{0,4},{3,1},{7,3},... | collective-permute-start | bytes 786440 | tf_op jit(solution)/shard_map/ppermute | solution.py:763
  151.3 8.9 %collective-permute-start.54 = (f32[512,128]{1,0:T(8,128)S(1)}, f32[512,128]{1,0:T(8,128)S(1)}, u32[]{:S(2)}, u32[]{:S(2)}) collective-permute-start(f32[512,128]{1,0:T(8,128)S(1)} %get-tuple-element.326), channel_id=1, source_target_pairs={{2,0},{6,2},{10,6},{14,10},{12,14},{8,12},{4,8},{0,4},{3,1},{7,3},... | collective-permute-start | bytes 786440 | tf_op jit(solution)/shard_map/ppermute | solution.py:763
  156.1 9.0 %collective-permute-start.39 = (f32[512,128]{1,0:T(8,128)S(1)}, f32[512,128]{1,0:T(8,128)S(1)}, u32[]{:S(2)}, u32[]{:S(2)}) collective-permute-start(f32[512,128]{1,0:T(8,128)S(1)} %get-tuple-element.304), channel_id=1, source_target_pairs={{0,2},{2,6},{6,10},{10,14},{14,12},{12,8},{8,4},{4,0},{1,3},{3,7},... | collective-permute-start | bytes 786440 | tf_op jit(solution)/shard_map/ppermute | solution.py:763
  156.9 9.2 %collective-permute-start.40 = (f32[512,128]{1,0:T(8,128)S(1)}, f32[512,128]{1,0:T(8,128)S(1)}, u32[]{:S(2)}, u32[]{:S(2)}) collective-permute-start(f32[512,128]{1,0:T(8,128)S(1)} %get-tuple-element.305), channel_id=1, source_target_pairs={{2,0},{6,2},{10,6},{14,10},{12,14},{8,12},{4,8},{0,4},{3,1},{7,3},... | collective-permute-start | bytes 786440 | tf_op jit(solution)/shard_map/ppermute | solution.py:763
  163.5 9.1 %collective-permute-start.56 = (f32[512,128]{1,0:T(8,128)S(1)}, f32[512,128]{1,0:T(8,128)S(1)}, u32[]{:S(2)}, u32[]{:S(2)}) collective-permute-start(f32[512,128]{1,0:T(8,128)S(1)} %get-tuple-element.329), channel_id=1, source_target_pairs={{2,0},{6,2},{10,6},{14,10},{12,14},{8,12},{4,8},{0,4},{3,1},{7,3},... | collective-permute-start | bytes 786440 | tf_op jit(solution)/shard_map/ppermute | solution.py:763
  168.0 9.2 %collective-permute-start.41 = (f32[512,128]{1,0:T(8,128)S(1)}, f32[512,128]{1,0:T(8,128)S(1)}, u32[]{:S(2)}, u32[]{:S(2)}) collective-permute-start(f32[512,128]{1,0:T(8,128)S(1)} %get-tuple-element.307), channel_id=1, source_target_pairs={{0,2},{2,6},{6,10},{10,14},{14,12},{12,8},{8,4},{4,0},{1,3},{3,7},... | collective-permute-start | bytes 786440 | tf_op jit(solution)/shard_map/ppermute | solution.py:763
  169.5 9.1 %collective-permute-start.42 = (f32[512,128]{1,0:T(8,128)S(1)}, f32[512,128]{1,0:T(8,128)S(1)}, u32[]{:S(2)}, u32[]{:S(2)}) collective-permute-start(f32[512,128]{1,0:T(8,128)S(1)} %get-tuple-element.308), channel_id=1, source_target_pairs={{2,0},{6,2},{10,6},{14,10},{12,14},{8,12},{4,8},{0,4},{3,1},{7,3},... | collective-permute-start | bytes 786440 | tf_op jit(solution)/shard_map/ppermute | solution.py:763
  174.5 9.1 %collective-permute-start.57 = (f32[512,128]{1,0:T(8,128)S(1)}, f32[512,128]{1,0:T(8,128)S(1)}, u32[]{:S(2)}, u32[]{:S(2)}) collective-permute-start(f32[512,128]{1,0:T(8,128)S(1)} %get-tuple-element.331), channel_id=1, source_target_pairs={{0,2},{2,6},{6,10},{10,14},{14,12},{12,8},{8,4},{4,0},{1,3},{3,7},... | collective-permute-start | bytes 786440 | tf_op jit(solution)/shard_map/ppermute | solution.py:763
  175.2 8.9 %collective-permute-start.58 = (f32[512,128]{1,0:T(8,128)S(1)}, f32[512,128]{1,0:T(8,128)S(1)}, u32[]{:S(2)}, u32[]{:S(2)}) collective-permute-start(f32[512,128]{1,0:T(8,128)S(1)} %get-tuple-element.332), channel_id=1, source_target_pairs={{2,0},{6,2},{10,6},{14,10},{12,14},{8,12},{4,8},{0,4},{3,1},{7,3},... | collective-permute-start | bytes 786440 | tf_op jit(solution)/shard_map/ppermute | solution.py:763
  180.5 9.0 %collective-permute-start.43 = (f32[512,128]{1,0:T(8,128)S(1)}, f32[512,128]{1,0:T(8,128)S(1)}, u32[]{:S(2)}, u32[]{:S(2)}) collective-permute-start(f32[512,128]{1,0:T(8,128)S(1)} %get-tuple-element.310), channel_id=1, source_target_pairs={{0,2},{2,6},{6,10},{10,14},{14,12},{12,8},{8,4},{4,0},{1,3},{3,7},... | collective-permute-start | bytes 786440 | tf_op jit(solution)/shard_map/ppermute | solution.py:763
  180.8 8.9 %collective-permute-start.44 = (f32[512,128]{1,0:T(8,128)S(1)}, f32[512,128]{1,0:T(8,128)S(1)}, u32[]{:S(2)}, u32[]{:S(2)}) collective-permute-start(f32[512,128]{1,0:T(8,128)S(1)} %get-tuple-element.311), channel_id=1, source_target_pairs={{2,0},{6,2},{10,6},{14,10},{12,14},{8,12},{4,8},{0,4},{3,1},{7,3},... | collective-permute-start | bytes 786440 | tf_op jit(solution)/shard_map/ppermute | solution.py:763
  186.0 9.1 %collective-permute-start.59 = (f32[512,128]{1,0:T(8,128)S(1)}, f32[512,128]{1,0:T(8,128)S(1)}, u32[]{:S(2)}, u32[]{:S(2)}) collective-permute-start(f32[512,128]{1,0:T(8,128)S(1)} %get-tuple-element.334), channel_id=1, source_target_pairs={{0,2},{2,6},{6,10},{10,14},{14,12},{12,8},{8,4},{4,0},{1,3},{3,7},... | collective-permute-start | bytes 786440 | tf_op jit(solution)/shard_map/ppermute | solution.py:763
  186.5 9.0 %collective-permute-start.60 = (f32[512,128]{1,0:T(8,128)S(1)}, f32[512,128]{1,0:T(8,128)S(1)}, u32[]{:S(2)}, u32[]{:S(2)}) collective-permute-start(f32[512,128]{1,0:T(8,128)S(1)} %get-tuple-element.335), channel_id=1, source_target_pairs={{2,0},{6,2},{10,6},{14,10},{12,14},{8,12},{4,8},{0,4},{3,1},{7,3},... | collective-permute-start | bytes 786440 | tf_op jit(solution)/shard_map/ppermute | solution.py:763
  191.7 9.1 %collective-permute-start.45 = (f32[512,128]{1,0:T(8,128)S(1)}, f32[512,128]{1,0:T(8,128)S(1)}, u32[]{:S(2)}, u32[]{:S(2)}) collective-permute-start(f32[512,128]{1,0:T(8,128)S(1)} %get-tuple-element.313), channel_id=1, source_target_pairs={{0,2},{2,6},{6,10},{10,14},{14,12},{12,8},{8,4},{4,0},{1,3},{3,7},... | collective-permute-start | bytes 786440 | tf_op jit(solution)/shard_map/ppermute | solution.py:763
  192.2 9.0 %collective-permute-start.46 = (f32[512,128]{1,0:T(8,128)S(1)}, f32[512,128]{1,0:T(8,128)S(1)}, u32[]{:S(2)}, u32[]{:S(2)}) collective-permute-start(f32[512,128]{1,0:T(8,128)S(1)} %get-tuple-element.314), channel_id=1, source_target_pairs={{2,0},{6,2},{10,6},{14,10},{12,14},{8,12},{4,8},{0,4},{3,1},{7,3},... | collective-permute-start | bytes 786440 | tf_op jit(solution)/shard_map/ppermute | solution.py:763
  197.3 8.9 %collective-permute-start.61 = (f32[512,128]{1,0:T(8,128)S(1)}, f32[512,128]{1,0:T(8,128)S(1)}, u32[]{:S(2)}, u32[]{:S(2)}) collective-permute-start(f32[512,128]{1,0:T(8,128)S(1)} %get-tuple-element.337), channel_id=1, source_target_pairs={{0,2},{2,6},{6,10},{10,14},{14,12},{12,8},{8,4},{4,0},{1,3},{3,7},... | collective-permute-start | bytes 786440 | tf_op jit(solution)/shard_map/ppermute | solution.py:763
  197.6 9.2 %collective-permute-start.62 = (f32[512,128]{1,0:T(8,128)S(1)}, f32[512,128]{1,0:T(8,128)S(1)}, u32[]{:S(2)}, u32[]{:S(2)}) collective-permute-start(f32[512,128]{1,0:T(8,128)S(1)} %get-tuple-element.338), channel_id=1, source_target_pairs={{2,0},{6,2},{10,6},{14,10},{12,14},{8,12},{4,8},{0,4},{3,1},{7,3},... | collective-permute-start | bytes 786440 | tf_op jit(solution)/shard_map/ppermute | solution.py:763
  202.9 8.9 %collective-permute-start.47 = (f32[512,128]{1,0:T(8,128)S(1)}, f32[512,128]{1,0:T(8,128)S(1)}, u32[]{:S(2)}, u32[]{:S(2)}) collective-permute-start(f32[512,128]{1,0:T(8,128)S(1)} %get-tuple-element.316), channel_id=1, source_target_pairs={{0,2},{2,6},{6,10},{10,14},{14,12},{12,8},{8,4},{4,0},{1,3},{3,7},... | collective-permute-start | bytes 786440 | tf_op jit(solution)/shard_map/ppermute | solution.py:763
  203.4 9.1 %collective-permute-start.48 = (f32[512,128]{1,0:T(8,128)S(1)}, f32[512,128]{1,0:T(8,128)S(1)}, u32[]{:S(2)}, u32[]{:S(2)}) collective-permute-start(f32[512,128]{1,0:T(8,128)S(1)} %get-tuple-element.317), channel_id=1, source_target_pairs={{2,0},{6,2},{10,6},{14,10},{12,14},{8,12},{4,8},{0,4},{3,1},{7,3},... | collective-permute-start | bytes 786440 | tf_op jit(solution)/shard_map/ppermute | solution.py:763
  208.6 13.4 %collective-permute-start.67 = (f32[512,128]{1,0:T(8,128)S(1)}, f32[512,128]{1,0:T(8,128)S(1)}, u32[]{:S(2)}, u32[]{:S(2)}) collective-permute-start(f32[512,128]{1,0:T(8,128)S(1)} %get-tuple-element.350), channel_id=1, source_target_pairs={{0,2},{2,6},{6,10},{10,14},{14,12},{12,8},{8,4},{4,0},{1,3},{3,7},... | collective-permute-start | bytes 786440 | tf_op jit(solution)/shard_map/ppermute | solution.py:763
  209.1 12.9 %collective-permute-start.68 = (f32[512,128]{1,0:T(8,128)S(1)}, f32[512,128]{1,0:T(8,128)S(1)}, u32[]{:S(2)}, u32[]{:S(2)}) collective-permute-start(f32[512,128]{1,0:T(8,128)S(1)} %get-tuple-element.351), channel_id=1, source_target_pairs={{2,0},{6,2},{10,6},{14,10},{12,14},{8,12},{4,8},{0,4},{3,1},{7,3},... | collective-permute-start | bytes 786440 | tf_op jit(solution)/shard_map/ppermute | solution.py:763
  214.3 12.5 %collective-permute-start.63 = (f32[512,128]{1,0:T(8,128)S(1)}, f32[512,128]{1,0:T(8,128)S(1)}, u32[]{:S(2)}, u32[]{:S(2)}) collective-permute-start(f32[512,128]{1,0:T(8,128)S(1)} %get-tuple-element.343), channel_id=1, source_target_pairs={{0,2},{2,6},{6,10},{10,14},{14,12},{12,8},{8,4},{4,0},{1,3},{3,7},... | collective-permute-start | bytes 786440 | tf_op jit(solution)/shard_map/ppermute | solution.py:763
  215.0 11.8 %collective-permute-start.64 = (f32[512,128]{1,0:T(8,128)S(1)}, f32[512,128]{1,0:T(8,128)S(1)}, u32[]{:S(2)}, u32[]{:S(2)}) collective-permute-start(f32[512,128]{1,0:T(8,128)S(1)} %get-tuple-element.344), channel_id=1, source_target_pairs={{2,0},{6,2},{10,6},{14,10},{12,14},{8,12},{4,8},{0,4},{3,1},{7,3},... | collective-permute-start | bytes 786440 | tf_op jit(solution)/shard_map/ppermute | solution.py:763
  224.0 9.9 %collective-permute-start.69 = (f32[512,128]{1,0:T(8,128)S(1)}, f32[512,128]{1,0:T(8,128)S(1)}, u32[]{:S(2)}, u32[]{:S(2)}) collective-permute-start(f32[512,128]{1,0:T(8,128)S(1)} %get-tuple-element.353), channel_id=1, source_target_pairs={{0,2},{2,6},{6,10},{10,14},{14,12},{12,8},{8,4},{4,0},{1,3},{3,7},... | collective-permute-start | bytes 786440 | tf_op jit(solution)/shard_map/ppermute | solution.py:763
  225.4 9.2 %collective-permute-start.70 = (f32[512,128]{1,0:T(8,128)S(1)}, f32[512,128]{1,0:T(8,128)S(1)}, u32[]{:S(2)}, u32[]{:S(2)}) collective-permute-start(f32[512,128]{1,0:T(8,128)S(1)} %get-tuple-element.354), channel_id=1, source_target_pairs={{2,0},{6,2},{10,6},{14,10},{12,14},{8,12},{4,8},{0,4},{3,1},{7,3},... | collective-permute-start | bytes 786440 | tf_op jit(solution)/shard_map/ppermute | solution.py:763
  228.7 9.8 %collective-permute-start.65 = (f32[512,128]{1,0:T(8,128)S(1)}, f32[512,128]{1,0:T(8,128)S(1)}, u32[]{:S(2)}, u32[]{:S(2)}) collective-permute-start(f32[512,128]{1,0:T(8,128)S(1)} %get-tuple-element.346), channel_id=1, source_target_pairs={{0,2},{2,6},{6,10},{10,14},{14,12},{12,8},{8,4},{4,0},{1,3},{3,7},... | collective-permute-start | bytes 786440 | tf_op jit(solution)/shard_map/ppermute | solution.py:763
  229.0 10.6 %collective-permute-start.66 = (f32[512,128]{1,0:T(8,128)S(1)}, f32[512,128]{1,0:T(8,128)S(1)}, u32[]{:S(2)}, u32[]{:S(2)}) collective-permute-start(f32[512,128]{1,0:T(8,128)S(1)} %get-tuple-element.347), channel_id=1, source_target_pairs={{2,0},{6,2},{10,6},{14,10},{12,14},{8,12},{4,8},{0,4},{3,1},{7,3},... | collective-permute-start | bytes 786440 | tf_op jit(solution)/shard_map/ppermute | solution.py:763
  236.4 12.7 %collective-permute-start.75 = (f32[512,128]{1,0:T(8,128)S(1)}, f32[512,128]{1,0:T(8,128)S(1)}, u32[]{:S(2)}, u32[]{:S(2)}) collective-permute-start(f32[512,128]{1,0:T(8,128)S(1)} %get-tuple-element.366), channel_id=1, source_target_pairs={{0,2},{2,6},{6,10},{10,14},{14,12},{12,8},{8,4},{4,0},{1,3},{3,7},... | collective-permute-start | bytes 786440 | tf_op jit(solution)/shard_map/ppermute | solution.py:763
  238.0 11.1 %collective-permute-start.76 = (f32[512,128]{1,0:T(8,128)S(1)}, f32[512,128]{1,0:T(8,128)S(1)}, u32[]{:S(2)}, u32[]{:S(2)}) collective-permute-start(f32[512,128]{1,0:T(8,128)S(1)} %get-tuple-element.367), channel_id=1, source_target_pairs={{2,0},{6,2},{10,6},{14,10},{12,14},{8,12},{4,8},{0,4},{3,1},{7,3},... | collective-permute-start | bytes 786440 | tf_op jit(solution)/shard_map/ppermute | solution.py:763
  241.4 11.7 %collective-permute-start.71 = (f32[512,128]{1,0:T(8,128)S(1)}, f32[512,128]{1,0:T(8,128)S(1)}, u32[]{:S(2)}, u32[]{:S(2)}) collective-permute-start(f32[512,128]{1,0:T(8,128)S(1)} %get-tuple-element.359), channel_id=1, source_target_pairs={{0,2},{2,6},{6,10},{10,14},{14,12},{12,8},{8,4},{4,0},{1,3},{3,7},... | collective-permute-start | bytes 786440 | tf_op jit(solution)/shard_map/ppermute | solution.py:763
  241.6 11.4 %collective-permute-start.72 = (f32[512,128]{1,0:T(8,128)S(1)}, f32[512,128]{1,0:T(8,128)S(1)}, u32[]{:S(2)}, u32[]{:S(2)}) collective-permute-start(f32[512,128]{1,0:T(8,128)S(1)} %get-tuple-element.360), channel_id=1, source_target_pairs={{2,0},{6,2},{10,6},{14,10},{12,14},{8,12},{4,8},{0,4},{3,1},{7,3},... | collective-permute-start | bytes 786440 | tf_op jit(solution)/shard_map/ppermute | solution.py:763
  254.8 9.9 %collective-permute-start.73 = (f32[512,128]{1,0:T(8,128)S(1)}, f32[512,128]{1,0:T(8,128)S(1)}, u32[]{:S(2)}, u32[]{:S(2)}) collective-permute-start(f32[512,128]{1,0:T(8,128)S(1)} %get-tuple-element.362), channel_id=1, source_target_pairs={{0,2},{2,6},{6,10},{10,14},{14,12},{12,8},{8,4},{4,0},{1,3},{3,7},... | collective-permute-start | bytes 786440 | tf_op jit(solution)/shard_map/ppermute | solution.py:763
  262.0 12.9 %collective-permute-start.81 = (f32[512,128]{1,0:T(8,128)}, f32[512,128]{1,0:T(8,128)}, u32[]{:S(2)}, u32[]{:S(2)}) collective-permute-start(f32[512,128]{1,0:T(8,128)} %get-tuple-element.378), channel_id=1, source_target_pairs={{0,2},{2,6},{6,10},{10,14},{14,12},{12,8},{8,4},{4,0},{1,3},{3,7},... | collective-permute-start | bytes 786440 | tf_op jit(solution)/shard_map/ppermute | solution.py:763
  264.7 10.2 %collective-permute-start.82 = (f32[512,128]{1,0:T(8,128)S(1)}, f32[512,128]{1,0:T(8,128)}, u32[]{:S(2)}, u32[]{:S(2)}) collective-permute-start(f32[512,128]{1,0:T(8,128)S(1)} %get-tuple-element.379), channel_id=1, source_target_pairs={{2,0},{6,2},{10,6},{14,10},{12,14},{8,12},{4,8},{0,4},{3,1},{7,3},... | collective-permute-start | bytes 786440 | tf_op jit(solution)/shard_map/ppermute | solution.py:763
  (23 other events, 157.3 us)
where the time goes:
time: 290 us; the launch traced here: 287 us
  Pallas kernels  133 us (46%)
  starting transfers between devices  85.2 us (29%)
  waiting for transfers between devices  61 us (21%)
  other arithmetic  4.01 us (1%)
    pallas_call x32, Pallas kernels, pack_call(): pl.pallas_call(functools.partial(pack_kernel, items, t if static else Non...  59.1 us
    ppermute x32, starting transfers between devices, travel(): lax.ppermute(sends[1], 'limb', ccw)  36.8 us
    ppermute x32, starting transfers between devices, travel(): lax.ppermute(sends[0], 'limb', cw)  31.9 us
    pallas_call x4, Pallas kernels, lower_call(): pl.pallas_call(functools.partial(lower_kernel, low, high, guess, specials...  23.3 us
    ppermute x14, waiting for transfers between devices, per_device(): hop = lambda x, ring: lax.ppermute(x, 'limb', ring)  21.3 us
    ppermute x32, waiting for transfers between devices, travel(): lax.ppermute(sends[1], 'limb', ccw)  17.3 us
    ppermute x32, waiting for transfers between devices, travel(): lax.ppermute(sends[0], 'limb', cw)  16.9 us
    ppermute x14, starting transfers between devices, per_device(): hop = lambda x, ring: lax.ppermute(x, 'limb', ring)  15.8 us
  transfers between devices with their start and end apart: 81, of which 42 were waited for; matrix products, arithmetic and copies ran while one was open for 2% of the time, Pallas kernels for 36%

commit v1 on v0

--- a/solution.py
+++ b/solution.py
@@ -732,14 +732,15 @@
         blocks += right + left
         lens += spans * 2
         steps += [-r, -r, r, r]
-        if r == 2:
-            right[1], left[1], order, slot, gain, scale, plan, rounds, comp = lax.optimization_barrier(
-                (right[1], left[1], order, slot, gain, scale, plan, rounds, comp)
-            )
     if n % 2 == 0:
-        blocks += [hop(right[0], cw), hop(left[1], ccw)]
+        right[0] = hop(right[0], cw)
+        left[1] = hop(left[1], ccw)
+        blocks += [right[0], left[1]]
         lens += spans
         steps += [n // 2, n // 2]
+    blocks[-1], order, slot, gain, scale, plan, rounds, comp = lax.optimization_barrier(
+        (blocks[-1], order, slot, gain, scale, plan, rounds, comp)
+    )
     srcs = jnp.asarray(
         np.array([[order_of[(pos_of[d] + s) % n] for s in steps] for d in range(n)], np.int32)
     )[me]

time: 290 us -> 287 us (0.990)
  waiting for transfers between devices: 61 us -> 55.4 us
    ppermute x32, waiting for transfers between devices: 16.9 us -> 12.1 us  [travel(): lax.ppermute(sends[0], 'limb', cw)]
    ppermute x32, starting transfers between devices: 31.9 us -> 36 us  [travel(): lax.ppermute(sends[0], 'limb', cw)]
  transfers between devices with their start and end apart: 81 -> 81, of which waited for: 42 -> 43; matrix products, arithmetic and copies ran while one was open for 2% -> 2% of each run, Pallas kernels for 36% -> 36%
where the time goes in v1:
time: 287 us; the launch traced here: 284 us
  Pallas kernels  134 us (47%)
  starting transfers between devices  86.6 us (30%)
  waiting for transfers between devices  55.4 us (19%)
  other arithmetic  4 us (1%)
    pallas_call x32, Pallas kernels, pack_call(): pl.pallas_call(functools.partial(pack_kernel, items, t if static else Non...  59.1 us
    ppermute x32, starting transfers between devices, travel(): lax.ppermute(sends[0], 'limb', cw)  36 us
    ppermute x32, starting transfers between devices, travel(): lax.ppermute(sends[1], 'limb', ccw)  34.6 us
    pallas_call x4, Pallas kernels, lower_call(): pl.pallas_call(functools.partial(lower_kernel, low, high, guess, specials...  23.3 us
    ppermute x32, waiting for transfers between devices, travel(): lax.ppermute(sends[1], 'limb', ccw)  19 us
    ppermute x14, waiting for transfers between devices, per_device(): hop = lambda x, ring: lax.ppermute(x, 'limb', ring)  18.8 us
    ppermute x14, starting transfers between devices, per_device(): hop = lambda x, ring: lax.ppermute(x, 'limb', ring)  15.4 us
    pallas_call x4, Pallas kernels, accum_call(): pl.pallas_call(functools.partial(accum_kernel, k, limbs, pad), in_specs=s...  15.2 us
  transfers between devices with their start and end apart: 81, of which 43 were waited for; matrix products, arithmetic and copies ran while one was open for 2% of the time, Pallas kernels for 36%

profile of v1, /device:TPU:0, one launch (start us, length us, event | category | flops | bytes accessed | tf_op | source)
XLA Modules:
  0.0 283.8 jit_solution(37992316394260689)
XLA Ops:
  0.1 3.4 %coef.2 = (f32[2,256,128]{2,1,0:T(8,128)S(1)}, bf16[2,2,256,256]{3,2,1,0:T(8,128)(2,1)S(1)}) custom-call(s32[32]{0:T(128)} %tw.3, s32[2]{0:T(128)S(1)} %pad_add_fusion.where.refs_2_, bf16[256,256]{1,0:T(8,128)(2,1)} %constant.43.clone.base_hi, bf16[256,256]{1,0:T(8,128)(2,1)} %constant.44.clone.base_lo, f32[2048,128]{1,0:T(8,128)} %bitcast.45), custom_call_target="tpu_custom_call" | custom-call | flops 1000000000 | bytes 1048576 | tf_op jit(solution)/shard_map/coef/pallas_call | solution.py:109
  3.5 3.4 %coef.3 = (f32[2,256,128]{2,1,0:T(8,128)S(1)}, bf16[4,2,256,256]{3,2,1,0:T(8,128)(2,1)S(1)}) custom-call(s32[32]{0:T(128)} %tw.3, s32[2]{0:T(128)S(1)} %pad_add_fusion.where.refs_2_, bf16[256,256]{1,0:T(8,128)(2,1)} %constant.43.clone.base_hi, bf16[256,256]{1,0:T(8,128)(2,1)} %constant.44.clone.base_lo, f32[2048,128]{1,0:T(8,128)} %bitcast.46, ...), custom_call_target="tpu_custom_call" | custom-call | flops 1000000000 | bytes 1048576 | tf_op jit(solution)/shard_map/coef/pallas_call | solution.py:109
  6.9 3.1 %collective-permute-start.4 = (f32[2,256,128]{2,1,0:T(8,128)S(1)}, f32[2,256,128]{2,1,0:T(8,128)S(1)}, u32[]{:S(2)}, u32[]{:S(2)}) collective-permute-start(f32[2,256,128]{2,1,0:T(8,128)S(1)} %get-tuple-element.225.refs_1_), channel_id=1, source_target_pairs={{2,0},{6,2},{10,6},{14,10},{12,14},{8,12},{4,8},{0,4},{3,1},{7,3},... | collective-permute-start | bytes 786440 | tf_op jit(solution)/shard_map/ppermute | solution.py:726
  10.0 2.0 collective-permute-start.9
  13.4 3.7 %collective-permute-done.4.refs_5_ = f32[2,256,128]{2,1,0:T(8,128)S(1)} collective-permute-done((f32[2,256,128]{2,1,0:T(8,128)S(1)}, f32[2,256,128]{2,1,0:T(8,128)S(1)}, u32[]{:S(2)}, u32[]{:S(2)}) %collective-permute-start.4) | collective-permute-done | bytes 262176 | tf_op jit(solution)/shard_map/ppermute | solution.py:726
  17.1 2.1 collective-permute-start.5
  19.4 5.4 %collective-permute-done.9.refs_3_ = f32[2,256,128]{2,1,0:T(8,128)S(1)} collective-permute-done((f32[2,256,128]{2,1,0:T(8,128)S(1)}, f32[2,256,128]{2,1,0:T(8,128)S(1)}, u32[]{:S(2)}, u32[]{:S(2)}) %collective-permute-start.9) | collective-permute-done | bytes 262176 | tf_op jit(solution)/shard_map/ppermute | solution.py:726
  24.8 2.0 collective-permute-start.13
  28.3 2.1 collective-permute-start.6
  31.3 4.7 %collective-permute-done.12.refs_7_ = f32[2,256,128]{2,1,0:T(8,128)S(1)} collective-permute-done((f32[2,256,128]{2,1,0:T(8,128)S(1)}, f32[2,256,128]{2,1,0:T(8,128)S(1)}, u32[]{:S(2)}, u32[]{:S(2)}) %collective-permute-start.12) | collective-permute-done | bytes 262176 | tf_op jit(solution)/shard_map/ppermute | solution.py:726
  36.0 2.0 collective-permute-start.16
  39.7 2.0 collective-permute-start.7
  43.3 5.7 %table.1 = (s32[8,128]{1,0:T(8,128)S(1)}, s32[1]{0:T(128)}, s32[4]{0:T(128)S(1)}) custom-call(s32[32]{0:T(128)S(1)} %select_reduce_fusion.order.refs_0_, s32[8]{0:T(128)} %constant.42.clone.pos, s32[1]{0:T(128)} %dynamic_slice.18.spot), custom_call_target="tpu_custom_call" | custom-call | tf_op jit(solution)/shard_map/table/pallas_call | solution.py:434
  51.6 3.7 %mix.1.own = f32[3,4,256,128]{3,2,1,0:T(8,128)S(1)} custom-call(s32[32]{0:T(128)S(1)} %select_reduce_fusion.order.refs_0_, s32[32]{0:T(128)} %refs_1_.7, s32[2]{0:T(128)S(1)} %pad_add_fusion.where.refs_2_, s32[16]{0:T(128)S(1)} %dynamic-slice_bitcast_fusion.srcs, f32[32,32]{1,0:T(8,128)} %refs_4_.7, f32[2,256,128]{2,1,0:T(8,128)S(1)} %get-tuple-element.235.refs_0_, ...), custom_call_target="tpu_custom_call" | custom-call | tf_op jit(solution)/shard_map/mix/pallas_call | solution.py:165
  55.4 3.4 %collective-permute-done.18.other = f32[3,4,256,128]{3,2,1,0:T(8,128)S(1)} collective-permute-done((f32[3,4,256,128]{3,2,1,0:T(8,128)S(1)}, f32[3,4,256,128]{3,2,1,0:T(8,128)S(1)}, u32[]{:S(2)}, u32[]{:S(2)}) %collective-permute-start.18) | collective-permute-done | bytes 1572896 | tf_op jit(solution)/shard_map/ppermute | solution.py:688
  58.7 5.5 %raise.1.raised = f32[4,2112,128]{2,1,0:T(8,128)S(1)} custom-call(s32[32]{0:T(128)} %refs_1_.7, s32[2]{0:T(128)S(1)} %pad_add_fusion.where.refs_2_, f32[3,4,256,128]{3,2,1,0:T(8,128)S(1)} %mix.1.own, f32[3,4,256,128]{3,2,1,0:T(8,128)S(1)} %collective-permute-done.18.other, bf16[4,2,256,256]{3,2,1,0:T(8,128)(2,1)S(1)} %get-tuple-element.232.mats.refs_7_, ...), custom_call_target="tpu_custom_call" | custom-call | tf_op jit(solution)/shard_map/raise/pallas_call | solution.py:222
  64.2 3.7 %accum.4 = (f32[2048,128]{1,0:T(8,128)S(1)}, f32[2048,128]{1,0:T(8,128)S(1)}, f32[2,2048,128]{2,1,0:T(8,128)S(1)}) custom-call(s32[1,4]{1,0:T(1,128)} %shifts.4, f32[4,2112,128]{2,1,0:T(8,128)S(1)} %raise.1.raised, f32[4,6,2048,128]{3,2,1,0:T(8,128)} %bitcast.31, f32[4,2048,128]{2,1,0:T(8,128)} %bitcast.35, f32[8,128]{1,0:T(8,128)S(1)} %broadcast_in_dim.50.gain), custom_call_target="tpu_custom_call" | custom-call | flops 100000000 | bytes 8388608 | tf_op jit(solution)/shard_map/accum/pallas_call | solution.py:295
  68.0 3.7 %emit.4 = (f32[32,512,128]{2,1,0:T(8,128)}, f32[32,512,128]{2,1,0:T(8,128)}) custom-call(s32[4]{0:T(128)S(1)} %dynamic_slice.15.slot, f32[2,2048,128]{2,1,0:T(8,128)S(1)} %get-tuple-element.238.acc, bf16[4,2,256,256]{3,2,1,0:T(8,128)(2,1)S(1)} %get-tuple-element.232.mats.refs_7_), custom_call_target="tpu_custom_call" | custom-call | flops 1000000000 | bytes 1048576 | tf_op jit(solution)/shard_map/emit/pallas_call | solution.py:343
  73.4 2.0 collective-permute-start.22
  77.3 2.0 collective-permute-start.20
  79.2 3.8 %accum.5 = (f32[2048,128]{1,0:T(8,128)S(1)}, f32[2048,128]{1,0:T(8,128)S(1)}, f32[2,2048,128]{2,1,0:T(8,128)S(1)}) custom-call(s32[1,4]{1,0:T(1,128)} %shifts.4, f32[4,2112,128]{2,1,0:T(8,128)S(1)} %raise.1.raised, f32[4,6,2048,128]{3,2,1,0:T(8,128)} %bitcast.32, f32[4,2048,128]{2,1,0:T(8,128)} %bitcast.36, ...), custom_call_target="tpu_custom_call", output_to_operand_aliasing={{0}: (5, {}), {1}: (6, {})} | custom-call | flops 100000000 | bytes 8388608 | tf_op jit(solution)/shard_map/accum/pallas_call | solution.py:295
  83.1 3.8 %emit.5 = (f32[32,512,128]{2,1,0:T(8,128)}, f32[32,512,128]{2,1,0:T(8,128)}) custom-call(s32[4]{0:T(128)S(1)} %dynamic_slice.15.slot, f32[2,2048,128]{2,1,0:T(8,128)S(1)} %get-tuple-element.248.acc, bf16[4,2,256,256]{3,2,1,0:T(8,128)(2,1)S(1)} %get-tuple-element.232.mats.refs_7_, ...), custom_call_target="tpu_custom_call", output_to_operand_aliasing={{0}: (3, {}), {1}: (4, {})} | custom-call | flops 1000000000 | bytes 1048576 | tf_op jit(solution)/shard_map/emit/pallas_call | solution.py:343
  88.7 2.0 collective-permute-start.24
  92.6 2.0 collective-permute-start.26
  94.6 3.8 %accum.6 = (f32[2048,128]{1,0:T(8,128)S(1)}, f32[2048,128]{1,0:T(8,128)S(1)}, f32[2,2048,128]{2,1,0:T(8,128)S(1)}) custom-call(s32[1,4]{1,0:T(1,128)} %shifts.4, f32[4,2112,128]{2,1,0:T(8,128)S(1)} %raise.1.raised, f32[4,6,2048,128]{3,2,1,0:T(8,128)} %bitcast.33, f32[4,2048,128]{2,1,0:T(8,128)} %bitcast.37, ...), custom_call_target="tpu_custom_call", output_to_operand_aliasing={{0}: (5, {}), {1}: (6, {})} | custom-call | flops 100000000 | bytes 8388608 | tf_op jit(solution)/shard_map/accum/pallas_call | solution.py:295
  98.4 1.9 pack.38
  102.4 1.9 pack.39
  106.3 3.8 %emit.6 = (f32[32,512,128]{2,1,0:T(8,128)}, f32[32,512,128]{2,1,0:T(8,128)}) custom-call(s32[4]{0:T(128)S(1)} %dynamic_slice.15.slot, f32[2,2048,128]{2,1,0:T(8,128)S(1)} %get-tuple-element.266.acc, bf16[4,2,256,256]{3,2,1,0:T(8,128)(2,1)S(1)} %get-tuple-element.232.mats.refs_7_, ...), custom_call_target="tpu_custom_call", output_to_operand_aliasing={{0}: (3, {}), {1}: (4, {})} | custom-call | flops 1000000000 | bytes 1048576 | tf_op jit(solution)/shard_map/emit/pallas_call | solution.py:343
  110.1 1.9 pack.40
  112.0 1.9 collective-permute-start.31
  114.7 1.9 pack.41
  116.5 2.2 collective-permute-start.33
  118.7 3.8 %accum.7 = (f32[2048,128]{1,0:T(8,128)S(1)}, f32[2048,128]{1,0:T(8,128)S(1)}, f32[2,2048,128]{2,1,0:T(8,128)S(1)}) custom-call(s32[1,4]{1,0:T(1,128)} %shifts.4, f32[4,2112,128]{2,1,0:T(8,128)S(1)} %raise.1.raised, f32[4,6,2048,128]{3,2,1,0:T(8,128)} %bitcast.34, f32[4,2048,128]{2,1,0:T(8,128)} %bitcast.38, ...), custom_call_target="tpu_custom_call", output_to_operand_aliasing={{0}: (5, {}), {1}: (6, {})} | custom-call | flops 100000000 | bytes 8388608 | tf_op jit(solution)/shard_map/accum/pallas_call | solution.py:295
  122.6 1.9 pack.42
  124.5 2.0 collective-permute-start.49
  126.7 1.9 pack.43
  128.6 1.8 collective-permute-start.35
  130.7 3.7 %emit.7 = (f32[32,512,128]{2,1,0:T(8,128)}, f32[32,512,128]{2,1,0:T(8,128)}) custom-call(s32[4]{0:T(128)S(1)} %dynamic_slice.15.slot, f32[2,2048,128]{2,1,0:T(8,128)S(1)} %get-tuple-element.289.acc, bf16[4,2,256,256]{3,2,1,0:T(8,128)(2,1)S(1)} %get-tuple-element.232.mats.refs_7_, ...), custom_call_target="tpu_custom_call", output_to_operand_aliasing={{0}: (3, {}), {1}: (4, {})} | custom-call | flops 1000000000 | bytes 1048576 | tf_op jit(solution)/shard_map/emit/pallas_call | solution.py:343
  134.4 1.9 pack.51
  136.5 1.9 collective-permute-start.52
  139.6 1.9 pack.44
  141.5 2.0 collective-permute-start.38
  145.5 1.9 pack.52
  151.1 1.9 pack.45
  156.8 1.9 pack.53
  162.7 1.9 pack.46
  168.8 1.9 pack.54
  173.2 1.8 collective-permute-done.42.refs_3_
  175.0 1.9 pack.47
  180.8 1.9 pack.55
  186.7 1.9 pack.48
  213.2 5.6 %lower.4 = (f32[2048,128]{1,0:T(8,128)S(1)}, f32[2048,128]{1,0:T(8,128)S(1)}, f32[32,512,128]{2,1,0:T(8,128)}, f32[32,512,128]{2,1,0:T(8,128)}) custom-call(s32[32]{0:T(128)S(1)} %select_reduce_fusion.order.refs_0_, s32[32]{0:T(128)} %refs_1_.7, s32[2]{0:T(128)S(1)} %pad_add_fusion.where.refs_2_, ...), custom_call_target="tpu_custom_call", output_to_operand_aliasing={{2}: (10, {}), {3}: (11, {})} | custom-call | flops 1000000000 | bytes 8388608 | tf_op jit(solution)/shard_map/lower/pallas_call | solution.py:655
  218.9 1.9 pack.60
  223.7 1.9 pack.58
  227.6 1.8 collective-permute-done.69.refs_2_
  232.9 2.5 collective-permute-start.75
  239.3 5.6 %lower.5 = (f32[2048,128]{1,0:T(8,128)S(1)}, f32[2048,128]{1,0:T(8,128)S(1)}, f32[32,512,128]{2,1,0:T(8,128)}, f32[32,512,128]{2,1,0:T(8,128)}) custom-call(s32[32]{0:T(128)S(1)} %select_reduce_fusion.order.refs_0_, s32[32]{0:T(128)} %refs_1_.7, s32[2]{0:T(128)S(1)} %pad_add_fusion.where.refs_2_, ...), custom_call_target="tpu_custom_call", output_to_operand_aliasing={{2}: (10, {}), {3}: (11, {})} | custom-call | flops 1000000000 | bytes 8388608 | tf_op jit(solution)/shard_map/lower/pallas_call | solution.py:655
  246.7 2.5 collective-permute-start.77
  255.6 2.1 pack.65
  257.8 3.6 %collective-permute-start.81 = (f32[512,128]{1,0:T(8,128)}, f32[512,128]{1,0:T(8,128)}, u32[]{:S(2)}, u32[]{:S(2)}) collective-permute-start(f32[512,128]{1,0:T(8,128)} %get-tuple-element.376), channel_id=1, source_target_pairs={{0,2},{2,6},{6,10},{10,14},{14,12},{12,8},{8,4},{4,0},{1,3},{3,7},... | collective-permute-start | bytes 786440 | tf_op jit(solution)/shard_map/ppermute | solution.py:764
  261.5 2.2 pack.63
  263.8 2.2 collective-permute-start.79
  266.0 5.6 %lower.6 = (f32[2048,128]{1,0:T(8,128)S(1)}, f32[2048,128]{1,0:T(8,128)S(1)}, f32[32,512,128]{2,1,0:T(8,128)}, f32[32,512,128]{2,1,0:T(8,128)}) custom-call(s32[32]{0:T(128)S(1)} %select_reduce_fusion.order.refs_0_, s32[32]{0:T(128)} %refs_1_.7, s32[2]{0:T(128)S(1)} %pad_add_fusion.where.refs_2_, ...), custom_call_target="tpu_custom_call", output_to_operand_aliasing={{2}: (10, {}), {3}: (11, {})} | custom-call | flops 1000000000 | bytes 8388608 | tf_op jit(solution)/shard_map/lower/pallas_call | solution.py:655
  273.4 6.4 %lower.7 = (f32[32,512,128]{2,1,0:T(8,128)}, f32[32,512,128]{2,1,0:T(8,128)}, f32[1024,128]{1,0:T(8,128)S(1)}, f32[1024,128]{1,0:T(8,128)S(1)}, f32[1024,128]{1,0:T(8,128)S(1)}, /*index=5*/f32[1024,128]{1,0:T(8,128)S(1)}) custom-call(s32[32]{0:T(128)S(1)} %select_reduce_fusion.order.refs_0_, ...), custom_call_target="tpu_custom_call", output_to_operand_aliasing={{0}: (10, {}), {1}: (11, {})} | custom-call | flops 1000000000 | bytes 8388608 | tf_op jit(solution)/shard_map/lower/pallas_call | solution.py:655
  (178 shorter events, 103.1 us)
Async XLA Ops:
  6.9 10.2 %collective-permute-start.4 = (f32[2,256,128]{2,1,0:T(8,128)S(1)}, f32[2,256,128]{2,1,0:T(8,128)S(1)}, u32[]{:S(2)}, u32[]{:S(2)}) collective-permute-start(f32[2,256,128]{2,1,0:T(8,128)S(1)} %get-tuple-element.225.refs_1_), channel_id=1, source_target_pairs={{2,0},{6,2},{10,6},{14,10},{12,14},{8,12},{4,8},{0,4},{3,1},{7,3},... | collective-permute-start | bytes 786440 | tf_op jit(solution)/shard_map/ppermute | solution.py:726
  10.0 9.2 %collective-permute-start.8 = (f32[2,256,128]{2,1,0:T(8,128)S(1)}, f32[2,256,128]{2,1,0:T(8,128)S(1)}, u32[]{:S(2)}, u32[]{:S(2)}) collective-permute-start(f32[2,256,128]{2,1,0:T(8,128)S(1)} %get-tuple-element.235.refs_0_), channel_id=1, source_target_pairs={{0,2},{2,6},{6,10},{10,14},{14,12},{12,8},{8,4},{4,0},{1,3},{3,7},... | collective-permute-start | bytes 786440 | tf_op jit(solution)/shard_map/ppermute | solution.py:726
  10.0 14.8 %collective-permute-start.9 = (f32[2,256,128]{2,1,0:T(8,128)S(1)}, f32[2,256,128]{2,1,0:T(8,128)S(1)}, u32[]{:S(2)}, u32[]{:S(2)}) collective-permute-start(f32[2,256,128]{2,1,0:T(8,128)S(1)} %get-tuple-element.225.refs_1_), channel_id=1, source_target_pairs={{0,2},{2,6},{6,10},{10,14},{14,12},{12,8},{8,4},{4,0},{1,3},{3,7},... | collective-permute-start | bytes 786440 | tf_op jit(solution)/shard_map/ppermute | solution.py:726
  12.0 12.8 %collective-permute-start.10 = (f32[2,256,128]{2,1,0:T(8,128)S(1)}, f32[2,256,128]{2,1,0:T(8,128)S(1)}, u32[]{:S(2)}, u32[]{:S(2)}) collective-permute-start(f32[2,256,128]{2,1,0:T(8,128)S(1)} %get-tuple-element.235.refs_0_), channel_id=1, source_target_pairs={{2,0},{6,2},{10,6},{14,10},{12,14},{8,12},{4,8},{0,4},{3,1},{7,3},... | collective-permute-start | bytes 786440 | tf_op jit(solution)/shard_map/ppermute | solution.py:726
  17.1 11.2 %collective-permute-start.5 = (f32[2,256,128]{2,1,0:T(8,128)S(1)}, f32[2,256,128]{2,1,0:T(8,128)S(1)}, u32[]{:S(2)}, u32[]{:S(2)}) collective-permute-start(f32[2,256,128]{2,1,0:T(8,128)S(1)} %collective-permute-done.4.refs_5_), channel_id=1, source_target_pairs={{2,0},{6,2},{10,6},{14,10},{12,14},{8,12},{4,8},{0,4},{3,1},{7,3},... | collective-permute-start | bytes 786440 | tf_op jit(solution)/shard_map/ppermute | solution.py:726
  19.2 11.2 %collective-permute-start.11 = (f32[2,256,128]{2,1,0:T(8,128)S(1)}, f32[2,256,128]{2,1,0:T(8,128)S(1)}, u32[]{:S(2)}, u32[]{:S(2)}) collective-permute-start(f32[2,256,128]{2,1,0:T(8,128)S(1)} %collective-permute-done.8.refs_2_), channel_id=1, source_target_pairs={{0,2},{2,6},{6,10},{10,14},{14,12},{12,8},{8,4},{4,0},{1,3},{3,7},... | collective-permute-start | bytes 786440 | tf_op jit(solution)/shard_map/ppermute | solution.py:726
  24.8 11.2 %collective-permute-start.12 = (f32[2,256,128]{2,1,0:T(8,128)S(1)}, f32[2,256,128]{2,1,0:T(8,128)S(1)}, u32[]{:S(2)}, u32[]{:S(2)}) collective-permute-start(f32[2,256,128]{2,1,0:T(8,128)S(1)} %collective-permute-done.9.refs_3_), channel_id=1, source_target_pairs={{0,2},{2,6},{6,10},{10,14},{14,12},{12,8},{8,4},{4,0},{1,3},{3,7},... | collective-permute-start | bytes 786440 | tf_op jit(solution)/shard_map/ppermute | solution.py:726
  24.8 11.2 %collective-permute-start.13 = (f32[2,256,128]{2,1,0:T(8,128)S(1)}, f32[2,256,128]{2,1,0:T(8,128)}, u32[]{:S(2)}, u32[]{:S(2)}) collective-permute-start(f32[2,256,128]{2,1,0:T(8,128)S(1)} %collective-permute-done.10.refs_4_), channel_id=1, source_target_pairs={{2,0},{6,2},{10,6},{14,10},{12,14},{8,12},{4,8},{0,4},{3,1},{7,3},... | collective-permute-start | bytes 786440 | tf_op jit(solution)/shard_map/ppermute | solution.py:726
  28.3 11.4 %collective-permute-start.6 = (f32[2,256,128]{2,1,0:T(8,128)S(1)}, f32[2,256,128]{2,1,0:T(8,128)}, u32[]{:S(2)}, u32[]{:S(2)}) collective-permute-start(f32[2,256,128]{2,1,0:T(8,128)S(1)} %collective-permute-done.5.refs_9_), channel_id=1, source_target_pairs={{2,0},{6,2},{10,6},{14,10},{12,14},{8,12},{4,8},{0,4},{3,1},{7,3},... | collective-permute-start | bytes 786440 | tf_op jit(solution)/shard_map/ppermute | solution.py:726
  30.4 11.3 %collective-permute-start.14 = (f32[2,256,128]{2,1,0:T(8,128)S(1)}, f32[2,256,128]{2,1,0:T(8,128)}, u32[]{:S(2)}, u32[]{:S(2)}) collective-permute-start(f32[2,256,128]{2,1,0:T(8,128)S(1)} %collective-permute-done.11.refs_6_), channel_id=1, source_target_pairs={{0,2},{2,6},{6,10},{10,14},{14,12},{12,8},{8,4},{4,0},{1,3},{3,7},... | collective-permute-start | bytes 786440 | tf_op jit(solution)/shard_map/ppermute | solution.py:726
  36.0 14.1 %collective-permute-start.15 = (f32[2,256,128]{2,1,0:T(8,128)S(1)}, f32[2,256,128]{2,1,0:T(8,128)}, u32[]{:S(2)}, u32[]{:S(2)}) collective-permute-start(f32[2,256,128]{2,1,0:T(8,128)S(1)} %collective-permute-done.12.refs_7_), channel_id=1, source_target_pairs={{0,2},{2,6},{6,10},{10,14},{14,12},{12,8},{8,4},{4,0},{1,3},{3,7},... | collective-permute-start | bytes 786440 | tf_op jit(solution)/shard_map/ppermute | solution.py:726
  36.0 14.1 %collective-permute-start.16 = (f32[2,256,128]{2,1,0:T(8,128)}, f32[2,256,128]{2,1,0:T(8,128)}, u32[]{:S(2)}, u32[]{:S(2)}) collective-permute-start(f32[2,256,128]{2,1,0:T(8,128)} %collective-permute-done.13.refs_8_), channel_id=1, source_target_pairs={{2,0},{6,2},{10,6},{14,10},{12,14},{8,12},{4,8},{0,4},{3,1},{7,3},... | collective-permute-start | bytes 786440 | tf_op jit(solution)/shard_map/ppermute | solution.py:726
  39.7 10.4 %collective-permute-start.7 = (f32[2,256,128]{2,1,0:T(8,128)}, f32[2,256,128]{2,1,0:T(8,128)}, u32[]{:S(2)}, u32[]{:S(2)}) collective-permute-start(f32[2,256,128]{2,1,0:T(8,128)} %collective-permute-done.6.refs_13_), channel_id=1, source_target_pairs={{2,0},{6,2},{10,6},{14,10},{12,14},{8,12},{4,8},{0,4},{3,1},{7,3},... | collective-permute-start | bytes 786440 | tf_op jit(solution)/shard_map/ppermute | solution.py:726
  41.7 9.8 %collective-permute-start.17 = (f32[2,256,128]{2,1,0:T(8,128)}, f32[2,256,128]{2,1,0:T(8,128)}, u32[]{:S(2)}, u32[]{:S(2)}) collective-permute-start(f32[2,256,128]{2,1,0:T(8,128)} %collective-permute-done.14.refs_10_), channel_id=1, source_target_pairs={{0,2},{2,6},{6,10},{10,14},{14,12},{12,8},{8,4},{4,0},{1,3},{3,7},... | collective-permute-start | bytes 786440 | tf_op jit(solution)/shard_map/ppermute | solution.py:726
  73.4 13.4 %collective-permute-start.21 = (f32[512,128]{1,0:T(8,128)S(1)}, f32[512,128]{1,0:T(8,128)S(1)}, u32[]{:S(2)}, u32[]{:S(2)}) collective-permute-start(f32[512,128]{1,0:T(8,128)S(1)} %get-tuple-element.242), channel_id=1, source_target_pairs={{0,2},{2,6},{6,10},{10,14},{14,12},{12,8},{8,4},{4,0},{1,3},{3,7},... | collective-permute-start | bytes 786440 | tf_op jit(solution)/shard_map/ppermute | solution.py:764
  73.4 13.4 %collective-permute-start.22 = (f32[512,128]{1,0:T(8,128)S(1)}, f32[512,128]{1,0:T(8,128)S(1)}, u32[]{:S(2)}, u32[]{:S(2)}) collective-permute-start(f32[512,128]{1,0:T(8,128)S(1)} %get-tuple-element.256), channel_id=1, source_target_pairs={{2,0},{6,2},{10,6},{14,10},{12,14},{8,12},{4,8},{0,4},{3,1},{7,3},... | collective-permute-start | bytes 786440 | tf_op jit(solution)/shard_map/ppermute | solution.py:764
  77.1 13.6 %collective-permute-start.19 = (f32[512,128]{1,0:T(8,128)S(1)}, f32[512,128]{1,0:T(8,128)S(1)}, u32[]{:S(2)}, u32[]{:S(2)}) collective-permute-start(f32[512,128]{1,0:T(8,128)S(1)} %get-tuple-element.252), channel_id=1, source_target_pairs={{0,2},{2,6},{6,10},{10,14},{14,12},{12,8},{8,4},{4,0},{1,3},{3,7},... | collective-permute-start | bytes 786440 | tf_op jit(solution)/shard_map/ppermute | solution.py:764
  77.3 13.5 %collective-permute-start.20 = (f32[512,128]{1,0:T(8,128)S(1)}, f32[512,128]{1,0:T(8,128)S(1)}, u32[]{:S(2)}, u32[]{:S(2)}) collective-permute-start(f32[512,128]{1,0:T(8,128)S(1)} %get-tuple-element.253), channel_id=1, source_target_pairs={{2,0},{6,2},{10,6},{14,10},{12,14},{8,12},{4,8},{0,4},{3,1},{7,3},... | collective-permute-start | bytes 786440 | tf_op jit(solution)/shard_map/ppermute | solution.py:764
  88.6 9.8 %collective-permute-start.23 = (f32[512,128]{1,0:T(8,128)S(1)}, f32[512,128]{1,0:T(8,128)S(1)}, u32[]{:S(2)}, u32[]{:S(2)}) collective-permute-start(f32[512,128]{1,0:T(8,128)S(1)} %get-tuple-element.257), channel_id=1, source_target_pairs={{0,2},{2,6},{6,10},{10,14},{14,12},{12,8},{8,4},{4,0},{1,3},{3,7},... | collective-permute-start | bytes 786440 | tf_op jit(solution)/shard_map/ppermute | solution.py:764
  88.7 9.7 %collective-permute-start.24 = (f32[512,128]{1,0:T(8,128)S(1)}, f32[512,128]{1,0:T(8,128)S(1)}, u32[]{:S(2)}, u32[]{:S(2)}) collective-permute-start(f32[512,128]{1,0:T(8,128)S(1)} %get-tuple-element.264), channel_id=1, source_target_pairs={{2,0},{6,2},{10,6},{14,10},{12,14},{8,12},{4,8},{0,4},{3,1},{7,3},... | collective-permute-start | bytes 786440 | tf_op jit(solution)/shard_map/ppermute | solution.py:764
  92.5 9.9 %collective-permute-start.25 = (f32[512,128]{1,0:T(8,128)S(1)}, f32[512,128]{1,0:T(8,128)S(1)}, u32[]{:S(2)}, u32[]{:S(2)}) collective-permute-start(f32[512,128]{1,0:T(8,128)S(1)} %get-tuple-element.268), channel_id=1, source_target_pairs={{0,2},{2,6},{6,10},{10,14},{14,12},{12,8},{8,4},{4,0},{1,3},{3,7},... | collective-permute-start | bytes 786440 | tf_op jit(solution)/shard_map/ppermute | solution.py:764
  92.6 9.8 %collective-permute-start.26 = (f32[512,128]{1,0:T(8,128)S(1)}, f32[512,128]{1,0:T(8,128)S(1)}, u32[]{:S(2)}, u32[]{:S(2)}) collective-permute-start(f32[512,128]{1,0:T(8,128)S(1)} %get-tuple-element.269), channel_id=1, source_target_pairs={{2,0},{6,2},{10,6},{14,10},{12,14},{8,12},{4,8},{0,4},{3,1},{7,3},... | collective-permute-start | bytes 786440 | tf_op jit(solution)/shard_map/ppermute | solution.py:764
  100.3 9.8 %collective-permute-start.27 = (f32[512,128]{1,0:T(8,128)S(1)}, f32[512,128]{1,0:T(8,128)S(1)}, u32[]{:S(2)}, u32[]{:S(2)}) collective-permute-start(f32[512,128]{1,0:T(8,128)S(1)} %get-tuple-element.265), channel_id=1, source_target_pairs={{0,2},{2,6},{6,10},{10,14},{14,12},{12,8},{8,4},{4,0},{1,3},{3,7},... | collective-permute-start | bytes 786440 | tf_op jit(solution)/shard_map/ppermute | solution.py:764
  101.1 9.0 %collective-permute-start.28 = (f32[512,128]{1,0:T(8,128)S(1)}, f32[512,128]{1,0:T(8,128)S(1)}, u32[]{:S(2)}, u32[]{:S(2)}) collective-permute-start(f32[512,128]{1,0:T(8,128)S(1)} %get-tuple-element.273), channel_id=1, source_target_pairs={{2,0},{6,2},{10,6},{14,10},{12,14},{8,12},{4,8},{0,4},{3,1},{7,3},... | collective-permute-start | bytes 786440 | tf_op jit(solution)/shard_map/ppermute | solution.py:764
  104.2 9.8 %collective-permute-start.29 = (f32[512,128]{1,0:T(8,128)S(1)}, f32[512,128]{1,0:T(8,128)S(1)}, u32[]{:S(2)}, u32[]{:S(2)}) collective-permute-start(f32[512,128]{1,0:T(8,128)S(1)} %get-tuple-element.281), channel_id=1, source_target_pairs={{0,2},{2,6},{6,10},{10,14},{14,12},{12,8},{8,4},{4,0},{1,3},{3,7},... | collective-permute-start | bytes 786440 | tf_op jit(solution)/shard_map/ppermute | solution.py:764
  105.5 9.1 %collective-permute-start.30 = (f32[512,128]{1,0:T(8,128)S(1)}, f32[512,128]{1,0:T(8,128)S(1)}, u32[]{:S(2)}, u32[]{:S(2)}) collective-permute-start(f32[512,128]{1,0:T(8,128)S(1)} %get-tuple-element.282), channel_id=1, source_target_pairs={{2,0},{6,2},{10,6},{14,10},{12,14},{8,12},{4,8},{0,4},{3,1},{7,3},... | collective-permute-start | bytes 786440 | tf_op jit(solution)/shard_map/ppermute | solution.py:764
  112.0 10.6 %collective-permute-start.31 = (f32[512,128]{1,0:T(8,128)S(1)}, f32[512,128]{1,0:T(8,128)S(1)}, u32[]{:S(2)}, u32[]{:S(2)}) collective-permute-start(f32[512,128]{1,0:T(8,128)S(1)} %get-tuple-element.274), channel_id=1, source_target_pairs={{0,2},{2,6},{6,10},{10,14},{14,12},{12,8},{8,4},{4,0},{1,3},{3,7},... | collective-permute-start | bytes 786440 | tf_op jit(solution)/shard_map/ppermute | solution.py:764
  113.8 8.7 %collective-permute-start.32 = (f32[512,128]{1,0:T(8,128)S(1)}, f32[512,128]{1,0:T(8,128)S(1)}, u32[]{:S(2)}, u32[]{:S(2)}) collective-permute-start(f32[512,128]{1,0:T(8,128)S(1)} %get-tuple-element.287), channel_id=1, source_target_pairs={{2,0},{6,2},{10,6},{14,10},{12,14},{8,12},{4,8},{0,4},{3,1},{7,3},... | collective-permute-start | bytes 786440 | tf_op jit(solution)/shard_map/ppermute | solution.py:764
  116.5 10.1 %collective-permute-start.33 = (f32[512,128]{1,0:T(8,128)S(1)}, f32[512,128]{1,0:T(8,128)S(1)}, u32[]{:S(2)}, u32[]{:S(2)}) collective-permute-start(f32[512,128]{1,0:T(8,128)S(1)} %get-tuple-element.291), channel_id=1, source_target_pairs={{0,2},{2,6},{6,10},{10,14},{14,12},{12,8},{8,4},{4,0},{1,3},{3,7},... | collective-permute-start | bytes 786440 | tf_op jit(solution)/shard_map/ppermute | solution.py:764
  124.5 9.9 %collective-permute-start.49 = (f32[512,128]{1,0:T(8,128)S(1)}, f32[512,128]{1,0:T(8,128)S(1)}, u32[]{:S(2)}, u32[]{:S(2)}) collective-permute-start(f32[512,128]{1,0:T(8,128)S(1)} %get-tuple-element.288), channel_id=1, source_target_pairs={{0,2},{2,6},{6,10},{10,14},{14,12},{12,8},{8,4},{4,0},{1,3},{3,7},... | collective-permute-start | bytes 786440 | tf_op jit(solution)/shard_map/ppermute | solution.py:764
  128.6 9.8 %collective-permute-start.35 = (f32[512,128]{1,0:T(8,128)S(1)}, f32[512,128]{1,0:T(8,128)S(1)}, u32[]{:S(2)}, u32[]{:S(2)}) collective-permute-start(f32[512,128]{1,0:T(8,128)S(1)} %get-tuple-element.296), channel_id=1, source_target_pairs={{0,2},{2,6},{6,10},{10,14},{14,12},{12,8},{8,4},{4,0},{1,3},{3,7},... | collective-permute-start | bytes 786440 | tf_op jit(solution)/shard_map/ppermute | solution.py:764
  130.4 9.2 %collective-permute-start.36 = (f32[512,128]{1,0:T(8,128)S(1)}, f32[512,128]{1,0:T(8,128)S(1)}, u32[]{:S(2)}, u32[]{:S(2)}) collective-permute-start(f32[512,128]{1,0:T(8,128)S(1)} %get-tuple-element.297), channel_id=1, source_target_pairs={{2,0},{6,2},{10,6},{14,10},{12,14},{8,12},{4,8},{0,4},{3,1},{7,3},... | collective-permute-start | bytes 786440 | tf_op jit(solution)/shard_map/ppermute | solution.py:764
  136.5 9.0 %collective-permute-start.52 = (f32[512,128]{1,0:T(8,128)S(1)}, f32[512,128]{1,0:T(8,128)S(1)}, u32[]{:S(2)}, u32[]{:S(2)}) collective-permute-start(f32[512,128]{1,0:T(8,128)S(1)} %get-tuple-element.321), channel_id=1, source_target_pairs={{2,0},{6,2},{10,6},{14,10},{12,14},{8,12},{4,8},{0,4},{3,1},{7,3},... | collective-permute-start | bytes 786440 | tf_op jit(solution)/shard_map/ppermute | solution.py:764
  141.5 9.6 %collective-permute-start.38 = (f32[512,128]{1,0:T(8,128)S(1)}, f32[512,128]{1,0:T(8,128)S(1)}, u32[]{:S(2)}, u32[]{:S(2)}) collective-permute-start(f32[512,128]{1,0:T(8,128)S(1)} %get-tuple-element.300), channel_id=1, source_target_pairs={{2,0},{6,2},{10,6},{14,10},{12,14},{8,12},{4,8},{0,4},{3,1},{7,3},... | collective-permute-start | bytes 786440 | tf_op jit(solution)/shard_map/ppermute | solution.py:764
  147.9 8.9 %collective-permute-start.54 = (f32[512,128]{1,0:T(8,128)S(1)}, f32[512,128]{1,0:T(8,128)S(1)}, u32[]{:S(2)}, u32[]{:S(2)}) collective-permute-start(f32[512,128]{1,0:T(8,128)S(1)} %get-tuple-element.324), channel_id=1, source_target_pairs={{2,0},{6,2},{10,6},{14,10},{12,14},{8,12},{4,8},{0,4},{3,1},{7,3},... | collective-permute-start | bytes 786440 | tf_op jit(solution)/shard_map/ppermute | solution.py:764
  153.5 9.2 %collective-permute-start.40 = (f32[512,128]{1,0:T(8,128)S(1)}, f32[512,128]{1,0:T(8,128)S(1)}, u32[]{:S(2)}, u32[]{:S(2)}) collective-permute-start(f32[512,128]{1,0:T(8,128)S(1)} %get-tuple-element.303), channel_id=1, source_target_pairs={{2,0},{6,2},{10,6},{14,10},{12,14},{8,12},{4,8},{0,4},{3,1},{7,3},... | collective-permute-start | bytes 786440 | tf_op jit(solution)/shard_map/ppermute | solution.py:764
  159.6 9.2 %collective-permute-start.56 = (f32[512,128]{1,0:T(8,128)S(1)}, f32[512,128]{1,0:T(8,128)S(1)}, u32[]{:S(2)}, u32[]{:S(2)}) collective-permute-start(f32[512,128]{1,0:T(8,128)S(1)} %get-tuple-element.327), channel_id=1, source_target_pairs={{2,0},{6,2},{10,6},{14,10},{12,14},{8,12},{4,8},{0,4},{3,1},{7,3},... | collective-permute-start | bytes 786440 | tf_op jit(solution)/shard_map/ppermute | solution.py:764
  166.1 8.9 %collective-permute-start.42 = (f32[512,128]{1,0:T(8,128)S(1)}, f32[512,128]{1,0:T(8,128)S(1)}, u32[]{:S(2)}, u32[]{:S(2)}) collective-permute-start(f32[512,128]{1,0:T(8,128)S(1)} %get-tuple-element.306), channel_id=1, source_target_pairs={{2,0},{6,2},{10,6},{14,10},{12,14},{8,12},{4,8},{0,4},{3,1},{7,3},... | collective-permute-start | bytes 786440 | tf_op jit(solution)/shard_map/ppermute | solution.py:764
  170.7 9.0 %collective-permute-start.57 = (f32[512,128]{1,0:T(8,128)S(1)}, f32[512,128]{1,0:T(8,128)S(1)}, u32[]{:S(2)}, u32[]{:S(2)}) collective-permute-start(f32[512,128]{1,0:T(8,128)S(1)} %get-tuple-element.329), channel_id=1, source_target_pairs={{0,2},{2,6},{6,10},{10,14},{14,12},{12,8},{8,4},{4,0},{1,3},{3,7},... | collective-permute-start | bytes 786440 | tf_op jit(solution)/shard_map/ppermute | solution.py:764
  171.7 9.2 %collective-permute-start.58 = (f32[512,128]{1,0:T(8,128)S(1)}, f32[512,128]{1,0:T(8,128)S(1)}, u32[]{:S(2)}, u32[]{:S(2)}) collective-permute-start(f32[512,128]{1,0:T(8,128)S(1)} %get-tuple-element.330), channel_id=1, source_target_pairs={{2,0},{6,2},{10,6},{14,10},{12,14},{8,12},{4,8},{0,4},{3,1},{7,3},... | collective-permute-start | bytes 786440 | tf_op jit(solution)/shard_map/ppermute | solution.py:764
  176.9 9.0 %collective-permute-start.43 = (f32[512,128]{1,0:T(8,128)S(1)}, f32[512,128]{1,0:T(8,128)S(1)}, u32[]{:S(2)}, u32[]{:S(2)}) collective-permute-start(f32[512,128]{1,0:T(8,128)S(1)} %get-tuple-element.308), channel_id=1, source_target_pairs={{0,2},{2,6},{6,10},{10,14},{14,12},{12,8},{8,4},{4,0},{1,3},{3,7},... | collective-permute-start | bytes 786440 | tf_op jit(solution)/shard_map/ppermute | solution.py:764
  177.5 9.2 %collective-permute-start.44 = (f32[512,128]{1,0:T(8,128)S(1)}, f32[512,128]{1,0:T(8,128)S(1)}, u32[]{:S(2)}, u32[]{:S(2)}) collective-permute-start(f32[512,128]{1,0:T(8,128)S(1)} %get-tuple-element.309), channel_id=1, source_target_pairs={{2,0},{6,2},{10,6},{14,10},{12,14},{8,12},{4,8},{0,4},{3,1},{7,3},... | collective-permute-start | bytes 786440 | tf_op jit(solution)/shard_map/ppermute | solution.py:764
  182.7 9.2 %collective-permute-start.59 = (f32[512,128]{1,0:T(8,128)S(1)}, f32[512,128]{1,0:T(8,128)S(1)}, u32[]{:S(2)}, u32[]{:S(2)}) collective-permute-start(f32[512,128]{1,0:T(8,128)S(1)} %get-tuple-element.332), channel_id=1, source_target_pairs={{0,2},{2,6},{6,10},{10,14},{14,12},{12,8},{8,4},{4,0},{1,3},{3,7},... | collective-permute-start | bytes 786440 | tf_op jit(solution)/shard_map/ppermute | solution.py:764
  183.5 9.2 %collective-permute-start.60 = (f32[512,128]{1,0:T(8,128)S(1)}, f32[512,128]{1,0:T(8,128)S(1)}, u32[]{:S(2)}, u32[]{:S(2)}) collective-permute-start(f32[512,128]{1,0:T(8,128)S(1)} %get-tuple-element.333), channel_id=1, source_target_pairs={{2,0},{6,2},{10,6},{14,10},{12,14},{8,12},{4,8},{0,4},{3,1},{7,3},... | collective-permute-start | bytes 786440 | tf_op jit(solution)/shard_map/ppermute | solution.py:764
  188.6 9.2 %collective-permute-start.45 = (f32[512,128]{1,0:T(8,128)S(1)}, f32[512,128]{1,0:T(8,128)S(1)}, u32[]{:S(2)}, u32[]{:S(2)}) collective-permute-start(f32[512,128]{1,0:T(8,128)S(1)} %get-tuple-element.311), channel_id=1, source_target_pairs={{0,2},{2,6},{6,10},{10,14},{14,12},{12,8},{8,4},{4,0},{1,3},{3,7},... | collective-permute-start | bytes 786440 | tf_op jit(solution)/shard_map/ppermute | solution.py:764
  189.6 9.2 %collective-permute-start.46 = (f32[512,128]{1,0:T(8,128)S(1)}, f32[512,128]{1,0:T(8,128)S(1)}, u32[]{:S(2)}, u32[]{:S(2)}) collective-permute-start(f32[512,128]{1,0:T(8,128)S(1)} %get-tuple-element.312), channel_id=1, source_target_pairs={{2,0},{6,2},{10,6},{14,10},{12,14},{8,12},{4,8},{0,4},{3,1},{7,3},... | collective-permute-start | bytes 786440 | tf_op jit(solution)/shard_map/ppermute | solution.py:764
  194.5 9.2 %collective-permute-start.61 = (f32[512,128]{1,0:T(8,128)S(1)}, f32[512,128]{1,0:T(8,128)S(1)}, u32[]{:S(2)}, u32[]{:S(2)}) collective-permute-start(f32[512,128]{1,0:T(8,128)S(1)} %get-tuple-element.335), channel_id=1, source_target_pairs={{0,2},{2,6},{6,10},{10,14},{14,12},{12,8},{8,4},{4,0},{1,3},{3,7},... | collective-permute-start | bytes 786440 | tf_op jit(solution)/shard_map/ppermute | solution.py:764
  195.3 9.2 %collective-permute-start.62 = (f32[512,128]{1,0:T(8,128)S(1)}, f32[512,128]{1,0:T(8,128)S(1)}, u32[]{:S(2)}, u32[]{:S(2)}) collective-permute-start(f32[512,128]{1,0:T(8,128)S(1)} %get-tuple-element.336), channel_id=1, source_target_pairs={{2,0},{6,2},{10,6},{14,10},{12,14},{8,12},{4,8},{0,4},{3,1},{7,3},... | collective-permute-start | bytes 786440 | tf_op jit(solution)/shard_map/ppermute | solution.py:764
  206.2 12.6 %collective-permute-start.67 = (f32[512,128]{1,0:T(8,128)S(1)}, f32[512,128]{1,0:T(8,128)S(1)}, u32[]{:S(2)}, u32[]{:S(2)}) collective-permute-start(f32[512,128]{1,0:T(8,128)S(1)} %get-tuple-element.348), channel_id=1, source_target_pairs={{0,2},{2,6},{6,10},{10,14},{14,12},{12,8},{8,4},{4,0},{1,3},{3,7},... | collective-permute-start | bytes 786440 | tf_op jit(solution)/shard_map/ppermute | solution.py:764
  206.5 12.4 %collective-permute-start.68 = (f32[512,128]{1,0:T(8,128)S(1)}, f32[512,128]{1,0:T(8,128)S(1)}, u32[]{:S(2)}, u32[]{:S(2)}) collective-permute-start(f32[512,128]{1,0:T(8,128)S(1)} %get-tuple-element.349), channel_id=1, source_target_pairs={{2,0},{6,2},{10,6},{14,10},{12,14},{8,12},{4,8},{0,4},{3,1},{7,3},... | collective-permute-start | bytes 786440 | tf_op jit(solution)/shard_map/ppermute | solution.py:764
  211.1 12.5 %collective-permute-start.63 = (f32[512,128]{1,0:T(8,128)S(1)}, f32[512,128]{1,0:T(8,128)S(1)}, u32[]{:S(2)}, u32[]{:S(2)}) collective-permute-start(f32[512,128]{1,0:T(8,128)S(1)} %get-tuple-element.341), channel_id=1, source_target_pairs={{0,2},{2,6},{6,10},{10,14},{14,12},{12,8},{8,4},{4,0},{1,3},{3,7},... | collective-permute-start | bytes 786440 | tf_op jit(solution)/shard_map/ppermute | solution.py:764
  212.1 11.6 %collective-permute-start.64 = (f32[512,128]{1,0:T(8,128)S(1)}, f32[512,128]{1,0:T(8,128)S(1)}, u32[]{:S(2)}, u32[]{:S(2)}) collective-permute-start(f32[512,128]{1,0:T(8,128)S(1)} %get-tuple-element.342), channel_id=1, source_target_pairs={{2,0},{6,2},{10,6},{14,10},{12,14},{8,12},{4,8},{0,4},{3,1},{7,3},... | collective-permute-start | bytes 786440 | tf_op jit(solution)/shard_map/ppermute | solution.py:764
  220.8 8.6 %collective-permute-start.69 = (f32[512,128]{1,0:T(8,128)S(1)}, f32[512,128]{1,0:T(8,128)S(1)}, u32[]{:S(2)}, u32[]{:S(2)}) collective-permute-start(f32[512,128]{1,0:T(8,128)S(1)} %get-tuple-element.351), channel_id=1, source_target_pairs={{0,2},{2,6},{6,10},{10,14},{14,12},{12,8},{8,4},{4,0},{1,3},{3,7},... | collective-permute-start | bytes 786440 | tf_op jit(solution)/shard_map/ppermute | solution.py:764
  225.6 9.8 %collective-permute-start.65 = (f32[512,128]{1,0:T(8,128)S(1)}, f32[512,128]{1,0:T(8,128)S(1)}, u32[]{:S(2)}, u32[]{:S(2)}) collective-permute-start(f32[512,128]{1,0:T(8,128)S(1)} %get-tuple-element.344), channel_id=1, source_target_pairs={{0,2},{2,6},{6,10},{10,14},{14,12},{12,8},{8,4},{4,0},{1,3},{3,7},... | collective-permute-start | bytes 786440 | tf_op jit(solution)/shard_map/ppermute | solution.py:764
  226.5 8.9 %collective-permute-start.66 = (f32[512,128]{1,0:T(8,128)S(1)}, f32[512,128]{1,0:T(8,128)S(1)}, u32[]{:S(2)}, u32[]{:S(2)}) collective-permute-start(f32[512,128]{1,0:T(8,128)S(1)} %get-tuple-element.345), channel_id=1, source_target_pairs={{2,0},{6,2},{10,6},{14,10},{12,14},{8,12},{4,8},{0,4},{3,1},{7,3},... | collective-permute-start | bytes 786440 | tf_op jit(solution)/shard_map/ppermute | solution.py:764
  232.9 12.1 %collective-permute-start.75 = (f32[512,128]{1,0:T(8,128)S(1)}, f32[512,128]{1,0:T(8,128)S(1)}, u32[]{:S(2)}, u32[]{:S(2)}) collective-permute-start(f32[512,128]{1,0:T(8,128)S(1)} %get-tuple-element.364), channel_id=1, source_target_pairs={{0,2},{2,6},{6,10},{10,14},{14,12},{12,8},{8,4},{4,0},{1,3},{3,7},... | collective-permute-start | bytes 786440 | tf_op jit(solution)/shard_map/ppermute | solution.py:764
  235.4 9.5 %collective-permute-start.76 = (f32[512,128]{1,0:T(8,128)S(1)}, f32[512,128]{1,0:T(8,128)S(1)}, u32[]{:S(2)}, u32[]{:S(2)}) collective-permute-start(f32[512,128]{1,0:T(8,128)S(1)} %get-tuple-element.365), channel_id=1, source_target_pairs={{2,0},{6,2},{10,6},{14,10},{12,14},{8,12},{4,8},{0,4},{3,1},{7,3},... | collective-permute-start | bytes 786440 | tf_op jit(solution)/shard_map/ppermute | solution.py:764
  237.2 12.7 %collective-permute-start.71 = (f32[512,128]{1,0:T(8,128)S(1)}, f32[512,128]{1,0:T(8,128)S(1)}, u32[]{:S(2)}, u32[]{:S(2)}) collective-permute-start(f32[512,128]{1,0:T(8,128)S(1)} %get-tuple-element.357), channel_id=1, source_target_pairs={{0,2},{2,6},{6,10},{10,14},{14,12},{12,8},{8,4},{4,0},{1,3},{3,7},... | collective-permute-start | bytes 786440 | tf_op jit(solution)/shard_map/ppermute | solution.py:764
  238.8 11.1 %collective-permute-start.72 = (f32[512,128]{1,0:T(8,128)S(1)}, f32[512,128]{1,0:T(8,128)S(1)}, u32[]{:S(2)}, u32[]{:S(2)}) collective-permute-start(f32[512,128]{1,0:T(8,128)S(1)} %get-tuple-element.358), channel_id=1, source_target_pairs={{2,0},{6,2},{10,6},{14,10},{12,14},{8,12},{4,8},{0,4},{3,1},{7,3},... | collective-permute-start | bytes 786440 | tf_op jit(solution)/shard_map/ppermute | solution.py:764
  246.7 8.7 %collective-permute-start.77 = (f32[512,128]{1,0:T(8,128)S(1)}, f32[512,128]{1,0:T(8,128)S(1)}, u32[]{:S(2)}, u32[]{:S(2)}) collective-permute-start(f32[512,128]{1,0:T(8,128)S(1)} %get-tuple-element.367), channel_id=1, source_target_pairs={{0,2},{2,6},{6,10},{10,14},{14,12},{12,8},{8,4},{4,0},{1,3},{3,7},... | collective-permute-start | bytes 786440 | tf_op jit(solution)/shard_map/ppermute | solution.py:764
  251.7 9.7 %collective-permute-start.73 = (f32[512,128]{1,0:T(8,128)S(1)}, f32[512,128]{1,0:T(8,128)S(1)}, u32[]{:S(2)}, u32[]{:S(2)}) collective-permute-start(f32[512,128]{1,0:T(8,128)S(1)} %get-tuple-element.360), channel_id=1, source_target_pairs={{0,2},{2,6},{6,10},{10,14},{14,12},{12,8},{8,4},{4,0},{1,3},{3,7},... | collective-permute-start | bytes 786440 | tf_op jit(solution)/shard_map/ppermute | solution.py:764
  252.9 8.7 %collective-permute-start.74 = (f32[512,128]{1,0:T(8,128)S(1)}, f32[512,128]{1,0:T(8,128)S(1)}, u32[]{:S(2)}, u32[]{:S(2)}) collective-permute-start(f32[512,128]{1,0:T(8,128)S(1)} %get-tuple-element.361), channel_id=1, source_target_pairs={{2,0},{6,2},{10,6},{14,10},{12,14},{8,12},{4,8},{0,4},{3,1},{7,3},... | collective-permute-start | bytes 786440 | tf_op jit(solution)/shard_map/ppermute | solution.py:764
  257.8 13.8 %collective-permute-start.81 = (f32[512,128]{1,0:T(8,128)}, f32[512,128]{1,0:T(8,128)}, u32[]{:S(2)}, u32[]{:S(2)}) collective-permute-start(f32[512,128]{1,0:T(8,128)} %get-tuple-element.376), channel_id=1, source_target_pairs={{0,2},{2,6},{6,10},{10,14},{14,12},{12,8},{8,4},{4,0},{1,3},{3,7},... | collective-permute-start | bytes 786440 | tf_op jit(solution)/shard_map/ppermute | solution.py:764
  261.4 10.2 %collective-permute-start.82 = (f32[512,128]{1,0:T(8,128)S(1)}, f32[512,128]{1,0:T(8,128)}, u32[]{:S(2)}, u32[]{:S(2)}) collective-permute-start(f32[512,128]{1,0:T(8,128)S(1)} %get-tuple-element.377), channel_id=1, source_target_pairs={{2,0},{6,2},{10,6},{14,10},{12,14},{8,12},{4,8},{0,4},{3,1},{7,3},... | collective-permute-start | bytes 786440 | tf_op jit(solution)/shard_map/ppermute | solution.py:764
  (23 other events, 158.9 us)
